TPU v7x, 32 devices: a whole 2x2x4 slice. The times are simulated.
32 devices in a mesh: dp: 8 (over z, y), tensor: 4 (over x, core).
Axes of the slice: x: 2, y: 2, z: 4, core: 2. Of those that a mesh axis runs over, the one named last changes fastest.
Arguments:
- tokens: bfloat16 [16384, 768], P('dp'), may hold values from -6 to 6
- segment_ids: int32 [8, 2048], P('dp'), may hold values from 0 to 3, never falling along the last dimension, each value on 1 to 1024 neighbouring positions
- live_lengths: int32 [8], P('dp'), may hold values from 1024 to 2048
- gain_one: float32 [768], replicated, may hold values from 0.25 to 1.75
- shift_one: float32 [768], replicated, may hold values from -3 to 3
- qkv_weight: bfloat16 [3, 768, 768], P(None, None, 'tensor'), may hold values from -0.21875 to 0.21875
- out_weight: bfloat16 [768, 768], P('tensor'), may hold values from -2 to 2
- gain_two: float32 [768], replicated, may hold values from 0.25 to 1.75
- shift_two: float32 [768], replicated, may hold values from -3 to 3
- up_weight: bfloat16 [768, 3072], P(None, 'tensor'), may hold values from -0.21875 to 0.21875
- down_weight: bfloat16 [3072, 768], P('tensor'), may hold values from -0.21875 to 0.21875
- grad_out: bfloat16 [16384, 768], P('dp'), may hold values from -6 to 6
Outputs:
- output: bfloat16 [16384, 768], P('dp')
- grad_tokens: bfloat16 [16384, 768], P('dp')
- grad_gain_one: float32 [768], replicated
- grad_shift_one: float32 [768], replicated
- grad_qkv: float32 [3, 768, 768], P(None, None, 'tensor')
- grad_out_weight: float32 [768, 768], P('tensor')
- grad_gain_two: float32 [768], replicated
- grad_shift_two: float32 [768], replicated
- grad_up: float32 [768, 3072], P(None, 'tensor')
- grad_down: float32 [3072, 768], P('tensor')
All inputs are finite; a program needn't handle non-finite values.
Results may differ from a plain program's by a relative error of at most 0.015.
Values may be sent and summed in bfloat16 or wider, within the bound.
No kernel may reach another device: no remote copies, remote signals or barrier semaphores. Data moves between devices by JAX's collectives and lax.ppermute only.
A program may use at most 128 MiB of HBM per device.

v0:
```python
from functools import partial

import jax
import jax.numpy as jnp
from jax import lax
from jax.sharding import PartitionSpec as P

HD = 64


def layer_norm(values, gain, shift):
    average = jnp.mean(values, -1, keepdims=True)
    centred = values - average
    spread = jnp.mean(centred * centred, -1, keepdims=True)
    return centred * lax.rsqrt(spread + 1e-05) * gain + shift


def local(
    tokens,
    segment_ids,
    live_lengths,
    gain_one,
    shift_one,
    qkv_weight,
    out_weight,
    gain_two,
    shift_two,
    up_weight,
    down_weight,
    grad_out,
):
    parts = lax.axis_size("tensor")
    inputs = tokens.astype(jnp.float32)
    length = inputs.shape[0]
    share = length // parts
    begin = lax.axis_index("tensor") * share
    input_share = lax.dynamic_slice_in_dim(inputs, begin, share, 0)
    grad_share = lax.dynamic_slice_in_dim(grad_out, begin, share, 0).astype(jnp.float32)
    gelu = partial(jax.nn.gelu, approximate=False)
    first = layer_norm(inputs, gain_one, shift_one).astype(jnp.bfloat16)
    mixed = jnp.einsum("td,cde->cte", first, qkv_weight, preferred_element_type=jnp.float32)
    query = (mixed[0] * 0.125).astype(jnp.bfloat16)
    keys = mixed[1].astype(jnp.bfloat16)
    values = mixed[2].astype(jnp.bfloat16)
    width = qkv_weight.shape[2]
    heads = width // HD
    key_heads = keys.reshape(length, heads, HD)
    value_heads = values.reshape(length, heads, HD)
    row_ids = segment_ids[0]
    live = live_lengths[0]
    block = min(512, length)
    count = length // block
    positions = jnp.arange(length, dtype=jnp.int32)

    def block_scores(index):
        start = index * block
        part = lax.dynamic_slice_in_dim(query, start, block, 0).reshape(block, heads, HD)
        own_ids = lax.dynamic_slice_in_dim(row_ids, start, block, 0)
        rows_at = start + jnp.arange(block, dtype=jnp.int32)
        allowed = (own_ids[:, None] == row_ids[None, :]) & (
            (positions[None, :] < live) | (positions[None, :] == rows_at[:, None])
        )
        scores = jnp.einsum("qhe,khe->hqk", part, key_heads, preferred_element_type=jnp.float32)
        return (part, jnp.where(allowed[None], scores, -1e30))

    def forward_block(index):
        part, scores = block_scores(index)
        row_max = jnp.max(scores, -1, keepdims=True)
        expos = jnp.exp(scores - row_max)
        totals = jnp.sum(expos, -1, keepdims=True)
        probs = (expos / totals).astype(jnp.bfloat16)
        result = jnp.einsum("hqk,khe->qhe", probs, value_heads, preferred_element_type=jnp.float32)
        return (result.reshape(block, width), (row_max + jnp.log(totals))[..., 0])

    attended, log_total = lax.map(forward_block, jnp.arange(count, dtype=jnp.int32))
    attended = attended.reshape(length, width).astype(jnp.bfloat16)
    middle_share = input_share + lax.psum_scatter(
        jnp.dot(attended, out_weight, preferred_element_type=jnp.float32),
        "tensor",
        scatter_dimension=0,
        tiled=True,
    )
    second = layer_norm(middle_share, gain_two, shift_two).astype(jnp.bfloat16)
    second_rows = lax.all_gather(second, "tensor", axis=0, tiled=True)
    pre_act = jnp.dot(second_rows, up_weight, preferred_element_type=jnp.float32)
    hidden = gelu(pre_act).astype(jnp.bfloat16)
    mlp_share = lax.psum_scatter(
        jnp.dot(
            lax.slice_in_dim(hidden, 0, share * lax.axis_size("tensor"), axis=0),
            down_weight,
            preferred_element_type=jnp.float32,
        ).astype(jnp.bfloat16),
        "tensor",
        scatter_dimension=0,
        tiled=True,
    ).astype(jnp.float32)
    output = lax.all_gather(
        (middle_share + mlp_share).astype(jnp.bfloat16), "tensor", axis=0, tiled=True
    )
    grad_down = jnp.einsum("tf,td->fd", hidden, grad_out, preferred_element_type=jnp.float32)
    grad_hidden = jnp.einsum("td,fd->tf", grad_out, down_weight, preferred_element_type=jnp.float32)
    grad_pre = jax.vjp(gelu, pre_act)[1](grad_hidden)[0].astype(jnp.bfloat16)
    grad_up = jnp.einsum("td,tf->df", second_rows, grad_pre, preferred_element_type=jnp.float32)
    grad_second = lax.psum_scatter(
        jnp.einsum("tf,df->td", grad_pre, up_weight, preferred_element_type=jnp.float32),
        "tensor",
        scatter_dimension=0,
        tiled=True,
    )
    grad_middle_norm, grad_gain_two, grad_shift_two = jax.vjp(
        layer_norm, middle_share, gain_two, shift_two
    )[1](grad_second)
    grad_middle = grad_share + grad_middle_norm
    grad_attn = lax.all_gather(grad_middle.astype(jnp.bfloat16), "tensor", axis=0, tiled=True)
    grad_out_weight = jnp.einsum(
        "te,td->ed", attended, grad_attn, preferred_element_type=jnp.float32
    )
    grad_attended = jnp.einsum(
        "td,ed->te", grad_attn, out_weight, preferred_element_type=jnp.float32
    ).astype(jnp.bfloat16)
    grad_heads = grad_attended.reshape(length, heads, HD)

    def backward_block(carry, index):
        key_grad, value_grad = carry
        part, scores = block_scores(index)
        probs = jnp.exp(scores - log_total[index][..., None])
        low_probs = probs.astype(jnp.bfloat16)
        grad_part = lax.dynamic_slice_in_dim(grad_heads, index * block, block, 0)
        value_grad = value_grad + jnp.einsum(
            "hqk,qhe->khe", low_probs, grad_part, preferred_element_type=jnp.float32
        )
        grad_probs = jnp.einsum(
            "qhe,khe->hqk", grad_part, value_heads, preferred_element_type=jnp.float32
        )
        inner = jnp.sum(probs * grad_probs, -1, keepdims=True)
        grad_scores = (probs * (grad_probs - inner)).astype(jnp.bfloat16)
        key_grad = key_grad + jnp.einsum(
            "hqk,qhe->khe", grad_scores, part, preferred_element_type=jnp.float32
        )
        query_grad = jnp.einsum(
            "hqk,khe->qhe", grad_scores, key_heads, preferred_element_type=jnp.float32
        )
        return ((key_grad, value_grad), query_grad.reshape(block, width))

    empty = jnp.zeros((length, heads, HD), jnp.float32)
    (key_grad, value_grad), query_grad = lax.scan(
        backward_block, (empty, empty), jnp.arange(count, dtype=jnp.int32)
    )
    grad_mixed = jnp.stack(
        [
            query_grad.reshape(length, width).astype(jnp.bfloat16) * jnp.bfloat16(0.125),
            key_grad.reshape(length, width).astype(jnp.bfloat16),
            value_grad.reshape(length, width).astype(jnp.bfloat16),
        ]
    )
    grad_qkv = jnp.einsum("td,cte->cde", first, grad_mixed, preferred_element_type=jnp.float32)
    grad_first = lax.psum_scatter(
        jnp.einsum(
            "cte,cde->td", grad_mixed, qkv_weight, preferred_element_type=jnp.float32
        ).astype(jnp.bfloat16),
        "tensor",
        scatter_dimension=0,
        tiled=True,
    ).astype(jnp.float32)
    grad_input_norm, grad_gain_one, grad_shift_one = jax.vjp(
        layer_norm, input_share, gain_one, shift_one
    )[1](grad_first)
    grad_tokens = lax.all_gather(
        (grad_middle + grad_input_norm).astype(jnp.bfloat16), "tensor", axis=0, tiled=True
    )
    grad_gain_one, grad_shift_one, grad_gain_two, grad_shift_two = lax.psum(
        (grad_gain_one, grad_shift_one, grad_gain_two, grad_shift_two), ("dp", "tensor")
    )
    grad_qkv, grad_out_weight, grad_up, grad_down = lax.psum(
        (grad_qkv, grad_out_weight, grad_up, grad_down), "dp"
    )
    return (
        output,
        grad_tokens,
        grad_gain_one,
        grad_shift_one,
        grad_qkv,
        grad_out_weight,
        grad_gain_two,
        grad_shift_two,
        grad_up,
        grad_down,
    )


def solution(mesh):
    in_specs = (
        P("dp", None),
        P("dp", None),
        P("dp"),
        P(),
        P(),
        P(None, None, "tensor"),
        P("tensor", None),
        P(),
        P(),
        P(None, "tensor"),
        P("tensor", None),
        P("dp", None),
    )
    out_specs = (
        P("dp", None),
        P("dp", None),
        P(),
        P(),
        P(None, None, "tensor"),
        P("tensor", None),
        P(),
        P(),
        P(None, "tensor"),
        P("tensor", None),
    )
    return jax.shard_map(local, mesh=mesh, in_specs=in_specs, out_specs=out_specs, check_vma=False)
```

profile of v0, /device:TPU:0, one launch (start us, length us, event | category | flops | bytes accessed | tf_op | source)
XLA Modules:
  0.0 898.1 jit_solution(12395318944038201735)
XLA Ops:
  18.0 104.0 %while.30 = (s32[]{:T(128)}, bf16[4,512,192]{1,2,0:T(8,128)(2,1)S(1)}, f32[4,3,512]{2,1,0:T(4,128)}, s32[4]{0:T(128)S(1)}, s32[2048]{0:T(1024)S(1)}, /*index=5*/...) while((s32[]{:T(128)}, ...), condition=%wide.region_5.6_spmd.clone.clone, body=%wide.region_2.5_spmd.clone.clone.sunk | while | flops 837813248 | bytes 44769504 | solution.py:75
  22.9 6.7 select_reduce_fusion.2
  29.6 7.8 fusion.120
  37.3 6.4 fusion.121
  48.8 6.7 select_reduce_fusion.2
  55.5 7.8 fusion.120
  63.2 6.4 fusion.121
  74.7 6.7 select_reduce_fusion.2
  81.3 7.8 fusion.120
  89.1 6.4 fusion.121
  100.6 6.7 select_reduce_fusion.2
  107.2 7.8 fusion.120
  115.0 6.4 fusion.121
  132.7 56.7 %reduce-scatter.5.cloned.1.call-done = f32[512,768]{1,0:T(8,128)} async-done(((f32[2048,768]{1,0:T(8,128)}), f32[512,768]{1,0:T(8,128)}) %reduce-scatter.5.cloned.1.call-update) | async-done | bytes 1572880 | tf_op jit(solution)/shard_map/reduce_scatter | solution.py:77
  194.8 28.4 %all-gather.5.cloned.1.call-done = bf16[2048,768]{1,0:T(8,128)(2,1)} async-done(((bf16[512,768]{1,0:T(8,128)(2,1)}), bf16[2048,768]{1,0:T(8,128)(2,1)}) %all-gather.5.cloned.1.call-update) | async-done | bytes 3145744 | tf_op jit(solution)/shard_map/all_gather | solution.py:84
  228.3 18.0 %add_convert_fusion = (bf16[2048,768]{1,0:T(8,128)(2,1)S(1)}, f32[2048,768]{1,0:T(8,128)}) fusion(f32[2048,768]{1,0:T(8,128)S(1)} %fusion.61, bf16[2048,768]{1,0:T(8,128)(2,1)S(1)} %copy-done.27, bf16[768,768]{1,0:T(8,128)(2,1)S(1)} %copy-done), kind=kOutput, calls=%fused_computation.45 | convolution fusion | flops 2529165312 | bytes 20054016 | tf_op jit(solution)/shard_map/td,fd->tf/dot_general | solution.py:101
  263.7 47.8 %reduce-scatter.9.cloned.1.call-done = f32[512,768]{1,0:T(8,128)} async-done(((f32[2048,768]{1,0:T(8,128)}), f32[512,768]{1,0:T(8,128)}) %reduce-scatter.9.cloned.1.call-update) | async-done | bytes 1572880 | tf_op jit(solution)/shard_map/reduce_scatter | solution.py:104
  314.6 37.8 %reduce-scatter.7.cloned.1.call-done = bf16[512,768]{1,0:T(8,128)(2,1)} async-done(((bf16[2048,768]{1,0:T(8,128)(2,1)}), bf16[512,768]{1,0:T(8,128)(2,1)}) %reduce-scatter.7.cloned.1.call-update) | async-done | bytes 786448 | tf_op jit(solution)/shard_map/reduce_scatter | solution.py:87
  359.5 28.6 %all-gather.9.cloned.1.call-done = bf16[2048,768]{1,0:T(8,128)(2,1)} async-done(((bf16[512,768]{1,0:T(8,128)(2,1)}), bf16[2048,768]{1,0:T(8,128)(2,1)}) %all-gather.9.cloned.1.call-update) | async-done | bytes 3145744 | tf_op jit(solution)/shard_map/all_gather | solution.py:114
  392.2 141.7 %while.31 = (s32[]{:T(128)}, f32[2048,3,64]{0,2,1:T(8,128)}, f32[2048,3,64]{0,2,1:T(8,128)}, bf16[4,512,192]{1,2,0:T(8,128)(2,1)}, s32[4]{0:T(128)S(1)}, /*index...) while((s32[]{:T(128)}, f32[2048,3,64]{0,2,1:T(8,128)}, ...), condition=%wide.region_15.16_spmd.clone.clone, body=%wide.region_13.15_spmd.clone.clone.sunk | while | flops 2056782848 | bytes 157288992 | solution.py:146
  544.0 37.2 %reduce-scatter.11.cloned.1.call-done = bf16[512,768]{1,0:T(8,128)(2,1)} async-done(((bf16[2048,768]{1,0:T(8,128)(2,1)}), bf16[512,768]{1,0:T(8,128)(2,1)}) %reduce-scatter.11.cloned.1.call-update) | async-done | bytes 786448 | tf_op jit(solution)/shard_map/reduce_scatter | solution.py:157
  589.4 7.7 fusion.65
  611.3 39.9 %all-reduce = (f32[768]{0:T(1024)}, f32[768]{0:T(1024)}, f32[768]{0:T(1024)}, f32[768]{0:T(1024)}) all-reduce(f32[768]{0:T(1024)S(1)} %get-tuple-element.277, f32[768]{0:T(1024)S(1)} %get-tuple-element.284, f32[768]{0:T(1024)S(1)} %copy-done.39, f32[768]{0:T(1024)S(1)} %copy-done.40), channel_id=1, replica_groups=mesh['dp'=8,'tensor'=4] {'dp','tensor'}, use_global_device_ids=true, to_apply=%region_22.23 | all-reduce | flops 3072 | bytes 24576 | tf_op jit(solution)/shard_map/psum | solution.py:171
  651.2 228.2 %all-reduce.4.cloned.1.call-done = (f32[3,768,192]{1,2,0:T(8,128)}, f32[192,768]{1,0:T(8,128)}, f32[768,768]{1,0:T(8,128)}, f32[768,768]{1,0:T(8,128)}) async-done(((f32[3,768,192]{1,2,0:T(8,128)}, f32[192,768]{1,0:T(8,128)}, f32[768,768]{1,0:T(8,128)}, f32[768,768]{1,0:T(8,128)}), (f32[3,768,192]{1,2,0:T(8,128)}, f32[192,768]{1,0:T(8,128)}, f32[768,768]{1,0:T(8,128)}, ...) | async-done | bytes 7077904 | tf_op jit(solution)/shard_map/psum | solution.py:174
  (316 shorter events, 255.2 us)
Async XLA Ops:
  7.2 221.1 %copy-start = (bf16[768,768]{1,0:T(8,128)(2,1)S(1)}, bf16[768,768]{1,0:T(8,128)(2,1)}, u32[]{:S(2)}) copy-start(bf16[768,768]{1,0:T(8,128)(2,1)} %param.26) | copy-start | bytes 3538948
  7.2 182.2 %reduce-scatter.5.cloned.1.call-start = ((), (), s32[]{:S(2)}) async-start(), calls=%async_computation.4 | async-start | bytes 7864320 | tf_op jit(solution)/shard_map/reduce_scatter | solution.py:77
  127.7 95.5 %all-gather.5.cloned.1.call-start = ((), (), s32[]{:S(2)}) async-start(), calls=%async_computation.5 | async-start | bytes 3932160 | tf_op jit(solution)/shard_map/all_gather | solution.py:84
  132.7 60.6 %copy-start.34 = (f32[768]{0:T(1024)S(1)}, f32[768]{0:T(1024)}, u32[]{:S(2)}) copy-start(f32[768]{0:T(1024)} %param.23) | copy-start | bytes 9220
  132.7 60.6 %copy-start.44 = (f32[768]{0:T(1024)S(1)}, f32[768]{0:T(1024)}, u32[]{:S(2)}) copy-start(f32[768]{0:T(1024)} %param.24) | copy-start | bytes 9220
  194.5 117.0 %reduce-scatter.9.cloned.1.call-start = ((), (), s32[]{:S(2)}) async-start(), calls=%async_computation.8 | async-start | bytes 7864320 | tf_op jit(solution)/shard_map/reduce_scatter | solution.py:104
  228.3 18.0 %copy-start.17 = (f32[2048,768]{1,0:T(8,128)}, f32[2048,768]{1,0:T(8,128)S(1)}, u32[]{:S(2)}) copy-start(f32[2048,768]{1,0:T(8,128)S(1)} %fusion.61) | copy-start | bytes 18874372
  228.3 19.7 %copy-start.46 = (bf16[768,768]{1,0:T(8,128)(2,1)S(1)}, bf16[768,768]{1,0:T(8,128)(2,1)}, u32[]{:S(2)}) copy-start(bf16[768,768]{1,0:T(8,128)(2,1)} %param.25) | copy-start | bytes 3538948
  252.5 99.9 %reduce-scatter.7.cloned.1.call-start = ((), (), s32[]{:S(2)}) async-start(), calls=%async_computation.6 | async-start | bytes 3932160 | tf_op jit(solution)/shard_map/reduce_scatter | solution.py:87
  263.7 124.4 %all-gather.9.cloned.1.call-start = ((), (), s32[]{:S(2)}) async-start(), calls=%async_computation.9 | async-start | bytes 3932160 | tf_op jit(solution)/shard_map/all_gather | solution.py:114
  356.0 32.1 %copy-start.31 = (bf16[192,768]{1,0:T(8,128)(2,1)S(1)}, bf16[192,768]{1,0:T(8,128)(2,1)}, u32[]{:S(2)}) copy-start(bf16[192,768]{1,0:T(8,128)(2,1)} %param.22) | copy-start | bytes 884740
  356.0 35.2 %copy-start.37 = (f32[512]{0:T(512)}, f32[512]{0:T(512)S(1)}, u32[]{:S(2)}) copy-start(f32[512]{0:T(512)S(1)} %negate_multiply_fusion.2) | copy-start | bytes 6148
  359.5 221.7 %reduce-scatter.11.cloned.1.call-start = ((), (), s32[]{:S(2)}) async-start(), calls=%async_computation.10 | async-start | bytes 3932160 | tf_op jit(solution)/shard_map/reduce_scatter | solution.py:157
  392.6 9.1 %copy-start.4 = (bf16[2048,3,64]{0,2,1:T(8,128)(2,1)}, bf16[2048,3,64]{0,2,1:T(8,128)(2,1)S(1)}, u32[]{:S(2)}) copy-start(bf16[2048,3,64]{0,2,1:T(8,128)(2,1)S(1)} %get-tuple-element.590) | copy-start | bytes 2359300 | tf_op jit(solution)/shard_map/while
  392.6 9.1 %copy-start.7 = (bf16[2048,3,64]{0,2,1:T(8,128)(2,1)}, bf16[2048,3,64]{0,2,1:T(8,128)(2,1)S(1)}, u32[]{:S(2)}) copy-start(bf16[2048,3,64]{0,2,1:T(8,128)(2,1)S(1)} %get-tuple-element.593) | copy-start | bytes 2359300 | tf_op jit(solution)/shard_map/while
  392.6 9.1 %copy-start.18 = (bf16[2048,3,64]{0,2,1:T(8,128)(2,1)}, bf16[2048,3,64]{0,2,1:T(8,128)(2,1)S(1)}, u32[]{:S(2)}) copy-start(bf16[2048,3,64]{0,2,1:T(8,128)(2,1)S(1)} %get-tuple-element.592) | copy-start | bytes 2359300 | tf_op jit(solution)/shard_map/while
  497.7 9.1 %copy-start.7 = (bf16[2048,3,64]{0,2,1:T(8,128)(2,1)}, bf16[2048,3,64]{0,2,1:T(8,128)(2,1)S(1)}, u32[]{:S(2)}) copy-start(bf16[2048,3,64]{0,2,1:T(8,128)(2,1)S(1)} %get-tuple-element.593) | copy-start | bytes 2359300 | tf_op jit(solution)/shard_map/while
  497.7 9.1 %copy-start.18 = (bf16[2048,3,64]{0,2,1:T(8,128)(2,1)}, bf16[2048,3,64]{0,2,1:T(8,128)(2,1)S(1)}, u32[]{:S(2)}) copy-start(bf16[2048,3,64]{0,2,1:T(8,128)(2,1)S(1)} %get-tuple-element.592) | copy-start | bytes 2359300 | tf_op jit(solution)/shard_map/while
  543.1 38.1 %copy-start.33 = (f32[768]{0:T(1024)S(1)}, f32[768]{0:T(1024)}, u32[]{:S(2)}) copy-start(f32[768]{0:T(1024)} %param.19) | copy-start | bytes 9220
  543.1 42.9 %copy-start.13 = (f32[512,768]{1,0:T(8,128)S(1)}, f32[512,768]{1,0:T(8,128)}, u32[]{:S(2)}) copy-start(f32[512,768]{1,0:T(8,128)} %copy-done.12) | copy-start | bytes 4718596
  543.2 42.9 %copy-start.38 = (f32[512]{0:T(512)S(1)}, f32[512]{0:T(512)}, u32[]{:S(2)}) copy-start(f32[512]{0:T(512)} %copy-done.37) | copy-start | bytes 6148
  543.2 68.1 %all-gather.7.cloned.1.call-start = ((), (), s32[]{:S(2)}) async-start(), calls=%async_computation.7 | async-start | bytes 3932160 | tf_op jit(solution)/shard_map/all_gather | solution.py:97
  543.9 107.2 %all-gather.11.cloned.1.call-start = ((), (), s32[]{:S(2)}) async-start(), calls=%async_computation.11 | async-start | bytes 3932160 | tf_op jit(solution)/shard_map/all_gather | solution.py:168
  589.3 290.0 %all-reduce.4.cloned.1.call-start = ((), (), s32[]{:S(2)}) async-start(), calls=%async_computation.12 | async-start | bytes 14155776 | tf_op jit(solution)/shard_map/psum | solution.py:174
  (62 other events, 248.2 us)
Sparse Core Ops, SparseCore 0:
  127.8 61.5 reduce-scatter.4
  194.7 28.4 all-gather.4
  252.6 58.8 reduce-scatter.8
  314.5 37.8 reduce-scatter.6
  359.6 28.4 all-gather.8
  543.3 37.8 reduce-scatter.10
  582.7 28.5 all-gather.6
  613.4 28.7 all-gather.10
  647.8 231.4 all-reduce.3
where the time goes:
time: 903 us; the launch traced here: 898 us
  waiting for transfers between devices  469 us (52%)
  matrix products  200 us (22%)
  other arithmetic  116 us (13%)
  local copies, waits for them, and re-layouts  43 us (5%)
  blocking collectives  39.9 us (4%)
  loops' own time  14.9 us (2%)
  between operations  14.6 us (2%)
    psum x1, waiting for transfers between devices, local(): lax.psum((grad_qkv, grad_out_weight, grad_up, grad_down), 'dp')  228 us
    reduce_scatter x1, waiting for transfers between devices, local(): lax.psum_scatter(jnp.dot(attended, out_weight, preferred_element_type=jnp...  56.7 us
    reduce_scatter x1, waiting for transfers between devices, local(): lax.psum_scatter(jnp.einsum('tf,df->td', grad_pre, up_weight, preferred_e...  47.8 us
    psum x1, blocking collectives, local(): lax.psum((grad_gain_one, grad_shift_one, grad_gain_two, grad_shift_two),...  39.9 us
    reduce_scatter x1, waiting for transfers between devices, local(): lax.psum_scatter(jnp.dot(lax.slice_in_dim(hidden, 0, share * lax.axis_siz...  37.8 us
    reduce_scatter x1, waiting for transfers between devices, local(): lax.psum_scatter(jnp.einsum('cte,cde->td', grad_mixed, qkv_weight, prefer...  37.2 us
    dot_general x8, matrix products, block_scores(): jnp.einsum('qhe,khe->hqk', part, key_heads, preferred_element_type=jnp.fl...  33.9 us
    reduce_sum x4, other arithmetic, forward_block(): totals = jnp.sum(expos, -1, keepdims=True)  31 us
  transfers between devices with their start and end apart: 9, of which 8 were waited for; matrix products, arithmetic and copies ran while one was open for 5% of the time, Pallas kernels for 0%

commit v1 on v0

v1 whole, which is shorter than its diff:
```python
from functools import partial

import jax
import jax.numpy as jnp
from jax import lax
from jax.experimental import pallas as pl
from jax.experimental.pallas import tpu as pltpu
from jax.sharding import PartitionSpec as P

HD = 64
LANES = 128
BLK = 256
BIG = 1e30
F32 = jnp.float32
BF16 = jnp.bfloat16
VMEM = pltpu.VMEM
SMEM = pltpu.SMEM
NN = (((1,), (0,)), ((), ()))
NT = (((1,), (1,)), ((), ()))
TN = (((0,), (0,)), ((), ()))


def mm(a, b, dims=NN):
    return lax.dot_general(a, b, dims, preferred_element_type=F32)


def normalized(values):
    average = jnp.mean(values, -1, keepdims=True)
    centred = values - average
    spread = jnp.mean(centred * centred, -1, keepdims=True)
    scale = lax.rsqrt(spread + 1e-05)
    return centred * scale, scale


def norm_back(e, n, scale):
    return (e - jnp.mean(e, -1, keepdims=True) - n * jnp.mean(e * n, -1, keepdims=True)) * scale


def front_kernel(live_ref, ids_ref, x_ref, gain_ref, shift_ref, w_ref,
                 first_ref, q_ref, k_ref, v_ref, info_ref, wp_ref):
    step = pl.program_id(0)

    @pl.when(step == 0)
    def _():
        ids = ids_ref[...]
        info_ref[0] = 0
        for s in range(1, 4):
            info_ref[s] = jnp.sum(jnp.where(ids < s, 1.0, 0.0)).astype(jnp.int32)
        info_ref[4] = ids.shape[1]
        info_ref[5] = live_ref[0]
        width = w_ref.shape[2]
        wp_ref[...] = jnp.zeros_like(wp_ref)
        wp_ref[:, :, 0:width] = w_ref[...]

    n, _ = normalized(x_ref[...].astype(F32))
    first = (n * gain_ref[...] + shift_ref[...]).astype(BF16)
    first_ref[...] = first
    rows = step * BLK + lax.broadcasted_iota(jnp.int32, (BLK, LANES), 0)
    lane = lax.broadcasted_iota(jnp.int32, (BLK, LANES), 1)
    low = jnp.zeros((BLK, LANES), jnp.int32)
    high = jnp.zeros((BLK, LANES), jnp.int32)
    for s in range(4):
        low = jnp.where(lane == HD + s, info_ref[s], low)
        high = jnp.where(lane == HD + s, info_ref[s + 1], high)
    inside = (rows >= low) & (rows < high)
    flag = lane == HD + 4
    in_ids = (lane >= HD) & (lane < HD + 4)
    q_ext = jnp.where(flag | (in_ids & ~inside), -BIG, 0.0)
    k_ext = jnp.where((in_ids & inside) | (flag & (rows >= info_ref[5])), 1.0, 0.0)
    v_ext = jnp.zeros((BLK, LANES), F32)
    own = lane < HD
    for c, (ref, ext) in enumerate(((q_ref, q_ext), (k_ref, k_ext), (v_ref, v_ext))):
        res = mm(first, wp_ref[c])
        if c == 0:
            res = res * 0.125
        pair = res[:, 0:LANES]
        for h, part in enumerate((pair, pltpu.roll(pair, HD, 1), res[:, LANES:2 * LANES])):
            ref[h] = jnp.where(own, part, ext).astype(BF16)


def front(live, ids, tokens, gain, shift, weight):
    length, dim = tokens.shape
    count = length // BLK
    heads = weight.shape[2] // HD
    full = lambda *shape: pl.BlockSpec(shape, lambda i: (0,) * len(shape))
    head_spec = pl.BlockSpec((heads, BLK, LANES), lambda i: (0, i, 0))
    head_shape = jax.ShapeDtypeStruct((heads, length, LANES), BF16)
    return pl.pallas_call(
        front_kernel,
        grid=(count,),
        in_specs=[
            pl.BlockSpec(memory_space=SMEM),
            full(1, length),
            pl.BlockSpec((BLK, dim), lambda i: (i, 0)),
            full(1, dim),
            full(1, dim),
            full(*weight.shape),
        ],
        out_specs=[
            pl.BlockSpec((BLK, dim), lambda i: (i, 0)),
            head_spec, head_spec, head_spec,
            pl.BlockSpec(memory_space=SMEM),
        ],
        out_shape=[
            jax.ShapeDtypeStruct((length, dim), BF16),
            head_shape, head_shape, head_shape,
            jax.ShapeDtypeStruct((8,), jnp.int32),
        ],
        scratch_shapes=[VMEM((3, dim, 2 * LANES), BF16)],
        name="front",
    )(live, ids, tokens, gain, shift, weight)


def segment_span(info_ref, first, last):
    low, high = jnp.int32(0), info_ref[4]
    for s in range(3, 0, -1):
        at = info_ref[s]
        high = jnp.where(at > last, at, high)
    for s in range(1, 4):
        at = info_ref[s]
        low = jnp.where(at <= first, at, low)
    return low, high


def diagonal_mask(scores, base, live):
    key = lax.broadcasted_iota(jnp.int32, scores.shape, 0)
    query = lax.broadcasted_iota(jnp.int32, scores.shape, 1)
    return jnp.where((key + base >= live) & (key != query), -BIG, scores)


def drop_flag(block):
    lane = lax.broadcasted_iota(jnp.int32, block.shape, 1)
    return jnp.where(lane == HD + 4, 0.0, block.astype(F32)).astype(BF16)


def attend_kernel(info_ref, q_ref, k_ref, v_ref, att_ref, lse_ref, vt_ref, acc_ref, max_ref):
    step = pl.program_id(0)
    heads, count = vt_ref.shape[0], vt_ref.shape[1]
    extra = vt_ref.shape[2] - HD

    @pl.when(step == 0)
    def _():
        one = jnp.where(lax.broadcasted_iota(jnp.int32, (extra, BLK), 0) == 0, 1.0, 0.0).astype(BF16)

        def fill(kb, _):
            rows = pl.ds(pl.multiple_of(kb * BLK, BLK), BLK)
            for h in range(heads):
                turned = jnp.transpose(v_ref[h, rows, :].astype(F32))
                vt_ref[h, kb, 0:HD, :] = turned[0:HD].astype(BF16)
                vt_ref[h, kb, HD:HD + extra, :] = one
            return 0
        lax.fori_loop(0, count, fill, 0)

    base = step * BLK
    live = info_ref[5]
    low, high = segment_span(info_ref, base, base + BLK - 1)
    rows = pl.ds(pl.multiple_of(base, BLK), BLK)
    for h in range(heads):
        scores = diagonal_mask(mm(k_ref[h, rows, :], drop_flag(q_ref[h]), NT), base, live)
        top = jnp.max(scores, 0, keepdims=True)
        probs = jnp.exp(scores - top).astype(BF16)
        acc_ref[h] = mm(vt_ref[h, step], probs)
        max_ref[h] = top

    begin = low // BLK
    end = (jnp.minimum(high, live) + (BLK - 1)) // BLK
    total = jnp.maximum(end - begin, 0)
    total = total - jnp.where((begin <= step) & (step < end), 1, 0)

    def body(t, _):
        kb = begin + t
        kb = kb + jnp.where(kb >= step, 1, 0)
        rows = pl.ds(pl.multiple_of(kb * BLK, BLK), BLK)
        for h in range(heads):
            scores = mm(k_ref[h, rows, :], q_ref[h], NT)
            old = max_ref[h]
            top = jnp.maximum(old, jnp.max(scores, 0, keepdims=True))
            probs = jnp.exp(scores - top).astype(BF16)
            acc_ref[h] = acc_ref[h] * jnp.exp(old - top) + mm(vt_ref[h, kb], probs)
            max_ref[h] = top
        return 0

    lax.fori_loop(0, total, body, 0)
    for h in range(heads):
        sums = acc_ref[h, HD:HD + 1, :]
        att_ref[h * HD:(h + 1) * HD, :] = (acc_ref[h, 0:HD, :] / sums).astype(BF16)
        lse_ref[0, h:h + 1, :] = max_ref[h] + jnp.log(sums)


def attend(info, q, k, v):
    heads, length, _ = q.shape
    count = length // BLK
    whole = pl.BlockSpec((heads, length, LANES), lambda i: (0, 0, 0))
    return pl.pallas_call(
        attend_kernel,
        grid=(count,),
        in_specs=[
            pl.BlockSpec(memory_space=SMEM),
            pl.BlockSpec((heads, BLK, LANES), lambda i: (0, i, 0)),
            whole, whole,
        ],
        out_specs=[
            pl.BlockSpec((heads * HD, BLK), lambda i: (0, i)),
            pl.BlockSpec((1, 8, BLK), lambda i: (i, 0, 0)),
        ],
        out_shape=[
            jax.ShapeDtypeStruct((heads * HD, length), BF16),
            jax.ShapeDtypeStruct((count, 8, BLK), F32),
        ],
        scratch_shapes=[
            VMEM((heads, count, HD + 16, BLK), BF16),
            VMEM((heads, HD + 16, BLK), F32),
            VMEM((heads, 1, BLK), F32),
        ],
        name="attend",
    )(info, q, k, v)


def attend_back_kernel(half_ref, info_ref, q_ref, k_ref, v_ref, att_ref, lse_ref, own_ref, other_ref,
                       dq_ref, dk_ref, dv_ref, dot_ref, do_ref, delta_ref, dqt_ref, kt_ref, dkv_ref):
    step = pl.program_id(0)
    heads, count = dqt_ref.shape[0], dqt_ref.shape[1]
    half = count // 2

    @pl.when(step == 0)
    def _():
        def fill(t, _):
            for place, ref in ((half_ref[0], own_ref), (1 - half_ref[0], other_ref)):
                qb = place * half + t
                for h in range(heads):
                    cols = pl.ds(pl.multiple_of(t * BLK, BLK), BLK)
                    part = ref[h * HD:(h + 1) * HD, cols].astype(F32)
                    at = pl.ds(pl.multiple_of(qb * BLK, BLK), BLK)
                    att = att_ref[h * HD:(h + 1) * HD, at].astype(F32)
                    delta_ref[qb, h:h + 1, :] = jnp.sum(part * att, 0, keepdims=True)
                    padded = jnp.concatenate([part, jnp.zeros_like(part)], 0)
                    dot_ref[h, qb] = padded.astype(BF16)
                    do_ref[h, qb] = jnp.transpose(padded).astype(BF16)
                    dqt_ref[h, qb] = jnp.zeros_like(dqt_ref[h, qb])
            return 0
        lax.fori_loop(0, half, fill, 0)

    base = step * BLK
    live = info_ref[5]
    low, high = segment_span(info_ref, base, base + BLK - 1)
    for h in range(heads):
        kt_ref[h] = jnp.transpose(k_ref[h].astype(F32))[0:HD].astype(BF16)

    def pair(qb, diagonal):
        rows = pl.ds(pl.multiple_of(qb * BLK, BLK), BLK)
        for h in range(heads):
            q = q_ref[h, rows, :]
            if diagonal:
                scores = diagonal_mask(mm(k_ref[h], drop_flag(q), NT), base, live)
            else:
                scores = mm(k_ref[h], q, NT)
            probs = jnp.exp(scores - lse_ref[qb, h:h + 1, :])
            grads = probs * (mm(v_ref[h], dot_ref[h, qb]) - delta_ref[qb, h:h + 1, :])
            probs, grads = probs.astype(BF16), grads.astype(BF16)
            dv = mm(probs, do_ref[h, qb])
            dk = mm(grads, q)
            if diagonal:
                dkv_ref[0, h] = dk
                dkv_ref[1, h] = dv
            else:
                dkv_ref[0, h] += dk
                dkv_ref[1, h] += dv
            dqt_ref[h, qb] += mm(kt_ref[h], grads)

    pair(step, True)
    begin = low // BLK
    end = (high + (BLK - 1)) // BLK
    total = jnp.where(base < live, end - begin - 1, 0)

    def body(t, _):
        qb = begin + t
        pair(qb + jnp.where(qb >= step, 1, 0), False)
        return 0

    lax.fori_loop(0, total, body, 0)
    lane = lax.broadcasted_iota(jnp.int32, (BLK, LANES), 1)
    for c, ref in enumerate((dk_ref, dv_ref)):
        two = jnp.where(lane < HD, dkv_ref[c, 0], pltpu.roll(dkv_ref[c, 1], HD, 1))
        ref[:, 0:LANES] = two.astype(BF16)
        ref[:, LANES:LANES + HD] = dkv_ref[c, 2][:, 0:HD].astype(BF16)

    @pl.when(step == count - 1)
    def _():
        def drain(qb, _):
            rows = pl.ds(pl.multiple_of(qb * BLK, BLK), BLK)
            two = jnp.concatenate([dqt_ref[0, qb], dqt_ref[1, qb]], 0)
            dq_ref[rows, 0:LANES] = (jnp.transpose(two) * 0.125).astype(BF16)
            last = jnp.concatenate([dqt_ref[2, qb], dqt_ref[2, qb]], 0)
            dq_ref[rows, LANES:LANES + HD] = (jnp.transpose(last) * 0.125)[:, 0:HD].astype(BF16)
            return 0
        lax.fori_loop(0, count, drain, 0)


def attend_back(half, info, q, k, v, att, lse, own, other):
    heads, length, _ = q.shape
    count = length // BLK
    width = heads * HD
    whole = pl.BlockSpec((heads, length, LANES), lambda i: (0, 0, 0))
    block = pl.BlockSpec((heads, BLK, LANES), lambda i: (0, i, 0))
    part = jax.ShapeDtypeStruct((length, width), BF16)
    return pl.pallas_call(
        attend_back_kernel,
        grid=(count,),
        in_specs=[
            pl.BlockSpec(memory_space=SMEM),
            pl.BlockSpec(memory_space=SMEM),
            whole, block, block,
            pl.BlockSpec((width, length), lambda i: (0, 0)),
            pl.BlockSpec((count, 8, BLK), lambda i: (0, 0, 0)),
            pl.BlockSpec((width, length // 2), lambda i: (0, 0)),
            pl.BlockSpec((width, length // 2), lambda i: (0, 0)),
        ],
        out_specs=[
            pl.BlockSpec((length, width), lambda i: (0, 0)),
            pl.BlockSpec((BLK, width), lambda i: (i, 0)),
            pl.BlockSpec((BLK, width), lambda i: (i, 0)),
        ],
        out_shape=[part, part, part],
        scratch_shapes=[
            VMEM((heads, count, LANES, BLK), BF16),
            VMEM((heads, count, BLK, LANES), BF16),
            VMEM((count, 8, BLK), F32),
            VMEM((heads, count, HD, BLK), F32),
            VMEM((heads, HD, BLK), BF16),
            VMEM((2, heads, BLK, LANES), F32),
        ],
        name="attend_back",
    )(half, info, q, k, v, att, lse, own, other)


def middle_kernel(half_ref, a0, a1, a2, a3, w0, w1, w2, w3, x_ref, go_ref, gain_ref, shift_ref, up_ref, down_ref,
                  *refs):
    second_ref, hidden_ref, pre_ref, out_ref, gs_ref, mid_ref = refs[-6:]
    proj = mm(a0[...], w0[...], TN)
    for a, w in ((a1, w1), (a2, w2), (a3, w3)):
        proj = proj + mm(a[...], w[...], TN)
    middle = x_ref[...].astype(F32) + proj
    mid_ref[...] = middle
    n, _ = normalized(middle)
    second = (n * gain_ref[...] + shift_ref[...]).astype(BF16)
    second_ref[...] = second
    pre = mm(second, up_ref[...])
    phi = 0.5 + 0.5 * lax.erf(pre * 0.7071067811865476)
    hidden = (pre * phi).astype(BF16)
    hidden_ref[...] = hidden
    slope = phi + pre * (0.3989422804014327 * jnp.exp(-0.5 * pre * pre))
    grad_pre = (mm(go_ref[...], down_ref[...], NT) * slope).astype(BF16)
    pre_ref[...] = grad_pre
    out_ref[...] = (0.25 * middle + mm(hidden, down_ref[...])).astype(BF16)
    gs_ref[...] = mm(grad_pre, up_ref[...], NT).astype(BF16)


def middle_part(place, att, weights, tokens, grad_out, gain, shift, up, down, carried):
    length, dim = tokens.shape
    width = att[0].shape[0]
    steps = length // BLK // 2
    rows = pl.BlockSpec((BLK, dim), lambda i, p: (p[0] * steps + i, 0))
    local = pl.BlockSpec((BLK, dim), lambda i, p: (i, 0))
    fixed = lambda *shape: pl.BlockSpec(shape, lambda i, p: (0,) * len(shape))
    anywhere = pl.BlockSpec(memory_space=pl.ANY)
    hidden_dim = up.shape[1]
    full = lambda d: jax.ShapeDtypeStruct((length, d), BF16)
    part = lambda t: jax.ShapeDtypeStruct((length // 2, dim), t)
    first_alias = 1 + 4 + 4 + 6
    return pl.pallas_call(
        middle_kernel,
        grid_spec=pltpu.PrefetchScalarGridSpec(
            num_scalar_prefetch=1,
            grid=(steps,),
            in_specs=[pl.BlockSpec((width, BLK), lambda i, p: (0, p[0] * steps + i))] * 4
            + [fixed(width, dim)] * 4
            + [rows, rows, fixed(1, dim), fixed(1, dim), fixed(*up.shape), fixed(*down.shape)]
            + [anywhere] * len(carried),
            out_specs=[rows, rows, rows, local, local, local],
        ),
        out_shape=[full(dim), full(hidden_dim), full(hidden_dim), part(BF16), part(BF16), part(F32)],
        input_output_aliases={first_alias + i: i for i in range(len(carried))},
        name="middle",
    )(place, *att, *weights, tokens, grad_out, gain, shift, up, down, *carried)


def norm_two_kernel(half_ref, own_ref, other_ref, mid_ref, go_ref, gain_ref, w0, w1, w2, w3,
                    gm_ref, keep_ref, send_ref, sums_ref):
    @pl.when(pl.program_id(0) == 0)
    def _():
        sums_ref[...] = jnp.zeros_like(sums_ref)
    g = own_ref[...].astype(F32) + other_ref[...].astype(F32)
    n, scale = normalized(mid_ref[...])
    sums_ref[0:1, :] += jnp.sum(g * n, 0, keepdims=True)
    sums_ref[1:2, :] += jnp.sum(g, 0, keepdims=True)
    gm = (0.5 * go_ref[...].astype(F32) + norm_back(g * gain_ref[...], n, scale)).astype(BF16)
    gm_ref[...] = gm
    width = w0.shape[0]
    keep_ref[0:width, :] = mm(w0[...], gm, NT).astype(BF16)
    keep_ref[width:2 * width, :] = mm(w1[...], gm, NT).astype(BF16)
    send_ref[0:width, :] = mm(w2[...], gm, NT).astype(BF16)
    send_ref[width:2 * width, :] = mm(w3[...], gm, NT).astype(BF16)


def norm_two(place, own, other, middle, grad_out, gain, weights):
    rows, dim = own.shape
    width = weights[0].shape[0]
    steps = rows // BLK
    local = pl.BlockSpec((BLK, dim), lambda i, p: (i, 0))
    fixed = lambda *shape: pl.BlockSpec(shape, lambda i, p: (0,) * len(shape))
    cols = pl.BlockSpec((2 * width, BLK), lambda i, p: (0, i))
    return pl.pallas_call(
        norm_two_kernel,
        grid_spec=pltpu.PrefetchScalarGridSpec(
            num_scalar_prefetch=1,
            grid=(steps,),
            in_specs=[local, local, local, pl.BlockSpec((BLK, dim), lambda i, p: (p[0] * steps + i, 0)), fixed(1, dim)]
            + [fixed(width, dim)] * 4,
            out_specs=[local, cols, cols, fixed(8, dim)],
        ),
        out_shape=[
            jax.ShapeDtypeStruct((rows, dim), BF16),
            jax.ShapeDtypeStruct((2 * width, rows), BF16),
            jax.ShapeDtypeStruct((2 * width, rows), BF16),
            jax.ShapeDtypeStruct((8, dim), F32),
        ],
        name="norm_two",
    )(place, own, other, middle, grad_out, gain, *weights)


def first_grad_kernel(place_ref, dq_ref, dk_ref, dv_ref, w_ref, out_ref):
    total = mm(dq_ref[...], w_ref[0], NT)
    total = total + mm(dk_ref[...], w_ref[1], NT)
    out_ref[...] = (total + mm(dv_ref[...], w_ref[2], NT)).astype(BF16)


def first_grad(place, dq, dk, dv, weight):
    length, width = dq.shape
    dim = weight.shape[1]
    steps = length // BLK // 2
    rows = pl.BlockSpec((BLK, width), lambda i, p: (p[0] * steps + i, 0))
    return pl.pallas_call(
        first_grad_kernel,
        grid_spec=pltpu.PrefetchScalarGridSpec(
            num_scalar_prefetch=1,
            grid=(steps,),
            in_specs=[rows, rows, rows, pl.BlockSpec(weight.shape, lambda i, p: (0, 0, 0))],
            out_specs=pl.BlockSpec((BLK, dim), lambda i, p: (i, 0)),
        ),
        out_shape=jax.ShapeDtypeStruct((length // 2, dim), BF16),
        name="first_grad",
    )(place, dq, dk, dv, weight)


def norm_one_kernel(place_ref, own_ref, other_ref, x_ref, gm_ref, gain_ref, out_ref, sums_ref):
    @pl.when(pl.program_id(0) == 0)
    def _():
        sums_ref[...] = jnp.zeros_like(sums_ref)
    g = own_ref[...].astype(F32) + other_ref[...].astype(F32)
    n, scale = normalized(x_ref[...].astype(F32))
    sums_ref[0:1, :] += jnp.sum(g * n, 0, keepdims=True)
    sums_ref[1:2, :] += jnp.sum(g, 0, keepdims=True)
    out_ref[...] = (gm_ref[...].astype(F32) + norm_back(g * gain_ref[...], n, scale)).astype(BF16)


def norm_one(place, own, other, tokens, gm, gain):
    rows, dim = own.shape
    steps = rows // BLK
    local = pl.BlockSpec((BLK, dim), lambda i, p: (i, 0))
    fixed = lambda *shape: pl.BlockSpec(shape, lambda i, p: (0,) * len(shape))
    return pl.pallas_call(
        norm_one_kernel,
        grid_spec=pltpu.PrefetchScalarGridSpec(
            num_scalar_prefetch=1,
            grid=(steps,),
            in_specs=[local, local, pl.BlockSpec((BLK, dim), lambda i, p: (p[0] * steps + i, 0)), local, fixed(1, dim)],
            out_specs=[local, fixed(8, dim)],
        ),
        out_shape=[jax.ShapeDtypeStruct((rows, dim), BF16), jax.ShapeDtypeStruct((8, dim), F32)],
        name="norm_one",
    )(place, own, other, tokens, gm, gain)


def swap(value, distance):
    return lax.ppermute(value, "tensor", [(t, t ^ distance) for t in range(4)])


def add(a, b):
    return a.astype(F32) + b.astype(F32)


def both_halves(core, mine):
    other = swap(mine, 1)
    rows = mine.shape[0]
    full = jnp.zeros((2 * rows, mine.shape[1]), mine.dtype)
    full = lax.dynamic_update_slice(full, mine, (core * rows, 0))
    return lax.dynamic_update_slice(full, other, ((1 - core) * rows, 0))


def local(
    tokens,
    segment_ids,
    live_lengths,
    gain_one,
    shift_one,
    qkv_weight,
    out_weight,
    gain_two,
    shift_two,
    up_weight,
    down_weight,
    grad_out,
):
    core = lax.axis_index("tensor") % 2
    mine = jnp.full((1,), core, jnp.int32)
    theirs = 1 - mine
    row = lambda v: v.reshape(1, -1)
    w_sib = swap(out_weight, 1)
    w_far = swap(out_weight, 2)
    w_diag = swap(w_far, 1)
    weights = (out_weight, w_sib, w_far, w_diag)

    first, q, k, v, info = front(live_lengths, segment_ids, tokens, row(gain_one), row(shift_one), qkv_weight)
    att, lse = attend(info, q, k, v)
    att_far = swap(att, 2)
    att_sib = swap(att, 1)
    att_diag = swap(att_far, 1)
    atts = (att, att_sib, att_far, att_diag)

    args = (atts, weights, tokens, grad_out, row(gain_two), row(shift_two), up_weight, down_weight)
    second, hidden, grad_pre, out_theirs, gs_theirs, _ = middle_part(theirs, *args, ())
    gs_got = swap(gs_theirs, 1)
    second, hidden, grad_pre, out_mine, gs_mine, middle = middle_part(mine, *args, (second, hidden, grad_pre))
    grad_mid, keep, send, sums_two = norm_two(mine, gs_mine, gs_got, middle, grad_out, row(gain_two), weights)
    got = swap(send, 2)
    width = out_weight.shape[0]
    grad_att_own = add(keep[:width], got[:width]).astype(BF16)
    grad_att_sib = add(keep[width:], got[width:]).astype(BF16)
    grad_att_other = swap(grad_att_sib, 1)

    dq, dk, dv = attend_back(mine, info, q, k, v, att, lse, grad_att_own, grad_att_other)
    gf_got = swap(first_grad(theirs, dq, dk, dv, qkv_weight), 1)
    gf_mine = first_grad(mine, dq, dk, dv, qkv_weight)
    partial_tokens, sums_one = norm_one(mine, gf_mine, gf_got, tokens, grad_mid, row(gain_one))
    grad_tokens = both_halves(core, add(partial_tokens, swap(partial_tokens, 2)).astype(BF16))

    out_half = add(out_mine, swap(out_theirs, 1)).astype(BF16)
    output = both_halves(core, add(out_half, swap(out_half, 2)).astype(BF16))

    grad_down = jnp.einsum("tf,td->fd", hidden, grad_out, preferred_element_type=F32)
    grad_up = jnp.einsum("td,tf->df", second, grad_pre, preferred_element_type=F32)
    rows = tokens.shape[0] // 2
    pieces = [
        jnp.dot(lax.dynamic_slice_in_dim(a, core * rows, rows, 1), grad_mid, preferred_element_type=F32) for a in atts
    ]
    pieces = [p.astype(BF16) for p in pieces]
    own = add(pieces[0], swap(pieces[1], 1))
    far = add(pieces[2], swap(pieces[3], 1))
    grad_out_weight = own + swap(far.astype(BF16), 2).astype(F32)
    grad_qkv = jnp.stack([jnp.einsum("td,te->de", first, g, preferred_element_type=F32) for g in (dq, dk, dv)])

    grads = lax.psum(tuple(g.astype(BF16) for g in (grad_up, grad_down)), "dp")
    grad_up, grad_down = (g.astype(F32) for g in grads)
    grads = lax.psum(tuple(g.astype(BF16) for g in (grad_qkv, grad_out_weight)), "dp")
    grad_qkv, grad_out_weight = (g.astype(F32) for g in grads)
    sums = lax.psum(jnp.concatenate([sums_one[0:2], sums_two[0:2]], 0), ("dp", "tensor"))
    return (
        output,
        grad_tokens,
        sums[0],
        sums[1],
        grad_qkv,
        grad_out_weight,
        sums[2],
        sums[3],
        grad_up,
        grad_down,
    )


def solution(mesh):
    in_specs = (
        P("dp", None),
        P("dp", None),
        P("dp"),
        P(),
        P(),
        P(None, None, "tensor"),
        P("tensor", None),
        P(),
        P(),
        P(None, "tensor"),
        P("tensor", None),
        P("dp", None),
    )
    out_specs = (
        P("dp", None),
        P("dp", None),
        P(),
        P(),
        P(None, None, "tensor"),
        P("tensor", None),
        P(),
        P(),
        P(None, "tensor"),
        P("tensor", None),
    )
    return jax.shard_map(local, mesh=mesh, in_specs=in_specs, out_specs=out_specs, check_vma=False)
```

time: 903 us -> 373 us (0.41); the launches traced: 898 us -> 379 us
  waiting for transfers between devices: 469 us -> 112 us
  matrix products: 200 us -> 20 us
  Pallas kernels: 0 us -> 108 us
  other arithmetic: 116 us -> 15.9 us
  blocking collectives: 39.9 us -> 78.5 us
  local copies, waits for them, and re-layouts: 43 us -> 17.8 us
  loops' own time: 14.9 us -> 0 us
  starting transfers between devices: 0.55 us -> 11.8 us
    psum x1, waiting for transfers between devices: 228 us -> 28.1 us  [local(): lax.psum(tuple((g.astype(BF16) for g in (grad_qkv, grad_out_weight))), 'dp')]
    reduce_scatter x4 -> x0, waiting for transfers between devices: 179 us -> none  [the longest x1 56.7 us: local(): lax.psum_scatter(jnp.dot(attended, out_weight, preferred_element_type=jnp...]
    dot_general x39 -> x9, matrix products: 198 us -> 20 us  [the longest x1 6.72 us: local(): jnp.einsum('td,tf->df', second, grad_pre, preferred_element_type=F32)]
    pallas_call x0 -> x9, Pallas kernels: none -> 108 us  [the longest x2 28.8 us: middle_part(): pl.pallas_call(middle_kernel, grid_spec=pltpu.PrefetchScalarGridSpec(num_...]
    ppermute x0 -> x18, waiting for transfers between devices: none -> 84.2 us  [swap(): return lax.ppermute(value, 'tensor', [(t, t ^ distance) for t in range(4)])]
    all_gather x4 -> x0, waiting for transfers between devices: 61.1 us -> none  [the longest x1 28.6 us: local(): lax.all_gather(grad_middle.astype(jnp.bfloat16), 'tensor', axis=0, tiled=...]
    reduce_sum x12 -> x0, other arithmetic: 49.2 us -> none  [the longest x4 31 us: forward_block(): totals = jnp.sum(expos, -1, keepdims=True)]
    psum x1, blocking collectives: 39.9 us -> 78.5 us  [local(): lax.psum(jnp.concatenate([sums_one[0:2], sums_two[0:2]], 0), ('dp', 'tens...]
  transfers between devices with their start and end apart: 9 -> 19, of which waited for: 8 -> 7; matrix products, arithmetic and copies ran while one was open for 5% -> 11% of each run, Pallas kernels for 0% -> 16%
where the time goes in v1:
time: 373 us; the launch traced here: 379 us
  waiting for transfers between devices  112 us (30%)
  Pallas kernels  108 us (29%)
  blocking collectives  78.5 us (21%)
  matrix products  20 us (5%)
  local copies, waits for them, and re-layouts  17.8 us (5%)
  other arithmetic  15.9 us (4%)
  between operations  14.9 us (4%)
  starting transfers between devices  11.8 us (3%)
    ppermute x18, waiting for transfers between devices, swap(): return lax.ppermute(value, 'tensor', [(t, t ^ distance) for t in range(4)])  84.2 us
    psum x1, blocking collectives, local(): lax.psum(jnp.concatenate([sums_one[0:2], sums_two[0:2]], 0), ('dp', 'tens...  78.5 us
    pallas_call x2, Pallas kernels, middle_part(): pl.pallas_call(middle_kernel, grid_spec=pltpu.PrefetchScalarGridSpec(num_...  28.8 us
    psum x1, waiting for transfers between devices, local(): lax.psum(tuple((g.astype(BF16) for g in (grad_qkv, grad_out_weight))), 'dp')  28.1 us
    pallas_call x1, Pallas kernels, attend_back(): pl.pallas_call(attend_back_kernel, grid=(count,), in_specs=[pl.BlockSpec(...  22.4 us
    pallas_call x1, Pallas kernels, attend(): pl.pallas_call(attend_kernel, grid=(count,), in_specs=[pl.BlockSpec(memor...  22 us
    ppermute x18, starting transfers between devices, swap(): return lax.ppermute(value, 'tensor', [(t, t ^ distance) for t in range(4)])  11.7 us
    pallas_call x1, Pallas kernels, front(): pl.pallas_call(front_kernel, grid=(count,), in_specs=[pl.BlockSpec(memory...  10.4 us
  transfers between devices with their start and end apart: 19, of which 7 were waited for; matrix products, arithmetic and copies ran while one was open for 11% of the time, Pallas kernels for 16%

profile of v1, /device:TPU:0, one launch (start us, length us, event | category | flops | bytes accessed | tf_op | source)
XLA Modules:
  0.0 378.7 jit_solution(12249836344140612586)
XLA Ops:
  7.2 2.3 copy.25.w_ref
  12.7 10.4 %front.1 = (bf16[2048,768]{1,0:T(8,128)(2,1)}, bf16[3,2048,128]{2,1,0:T(8,128)(2,1)}, bf16[3,2048,128]{2,1,0:T(8,128)(2,1)}, bf16[3,2048,128]{2,1,0:T(8,128)(2,1)}, s32[8]{0:T(128)}) custom-call(s32[1]{0:T(128)S(6)} %copy.39.live_ref, s32[1,2048]{1,0:T(1,128)} %ids_ref.1, bf16[2048,768]{1,0:T(8,128)(2,1)} %x_ref.7, f32[1,768]{1,0:T(1,128)} %reshape.34.gain_ref, ...), custom_call_target="tpu_custom_call" | custom-call | tf_op jit(solution)/shard_map/front/pallas_call | solution.py:88
  23.1 22.0 %attend.1 = (bf16[192,2048]{1,0:T(8,128)(2,1)}, f32[8,8,256]{2,1,0:T(8,128)}) custom-call(s32[8]{0:T(128)} %get-tuple-element.37.info_ref, bf16[3,2048,128]{2,1,0:T(8,128)(2,1)} %get-tuple-element.38.q_ref, bf16[3,2048,128]{2,1,0:T(8,128)(2,1)} %get-tuple-element.39.k_ref, bf16[3,2048,128]{2,1,0:T(8,128)(2,1)} %get-tuple-element.40.v_ref), custom_call_target="tpu_custom_call" | custom-call | tf_op jit(solution)/shard_map/attend/pallas_call | solution.py:194
  45.1 3.0 collective-permute-start.1
  48.1 17.7 %collective-permute-done.1.a2 = bf16[192,2048]{1,0:T(8,128)(2,1)S(1)} collective-permute-done((bf16[192,2048]{1,0:T(8,128)(2,1)}, bf16[192,2048]{1,0:T(8,128)(2,1)S(1)}, u32[]{:S(2)}, u32[]{:S(2)}) %collective-permute-start.1) | collective-permute-done | bytes 786464 | tf_op jit(solution)/shard_map/ppermute | solution.py:485
  67.8 7.4 %collective-permute-done.4.w2 = bf16[192,768]{1,0:T(8,128)(2,1)S(1)} collective-permute-done((bf16[192,768]{1,0:T(8,128)(2,1)S(1)}, bf16[192,768]{1,0:T(8,128)(2,1)S(1)}, u32[]{:S(2)}, u32[]{:S(2)}) %collective-permute-start.4) | collective-permute-done | bytes 294944 | tf_op jit(solution)/shard_map/ppermute | solution.py:485
  78.7 14.3 %middle.2 = (bf16[2048,768]{1,0:T(8,128)(2,1)}, bf16[2048,768]{1,0:T(8,128)(2,1)}, bf16[2048,768]{1,0:T(8,128)(2,1)}, bf16[1024,768]{1,0:T(8,128)(2,1)}, bf16[1024,768]{1,0:T(8,128)(2,1)}, /*index=5*/f32[1024,768]{1,0:T(8,128)}) custom-call(s32[1]{0:T(128)S(6)} %sub.7.half_ref.place_ref, bf16[192,2048]{1,0:T(8,128)(2,1)} %get-tuple-element.41.a0.att_ref, ...), custom_call_target="tpu_custom_call" | custom-call | tf_op jit(solution)/shard_map/middle/pallas_call | solution.py:370
  93.7 14.4 %middle.3 = (bf16[2048,768]{1,0:T(8,128)(2,1)}, bf16[2048,768]{1,0:T(8,128)(2,1)}, bf16[2048,768]{1,0:T(8,128)(2,1)}, bf16[1024,768]{1,0:T(8,128)(2,1)}, bf16[1024,768]{1,0:T(8,128)(2,1)}, /*index=5*/f32[1024,768]{1,0:T(8,128)}) custom-call(s32[1]{0:T(128)} %bitcast.half_ref.place_ref, ...), custom_call_target="tpu_custom_call", output_to_operand_aliasing={{0}: (15, {}), {1}: (16, {}), {2}: (17, {})} | custom-call | tf_op jit(solution)/shard_map/middle/pallas_call | solution.py:370
  108.1 5.6 %convolution_convert_fusion = bf16[768,768]{1,0:T(8,128)(2,1)} fusion(bf16[2048,768]{1,0:T(8,128)(2,1)} %get-tuple-element.63, bf16[2048,768]{1,0:T(8,128)(2,1)S(1)} %copy-done.1), kind=kOutput, calls=%fused_computation.3 | convolution fusion | flops 2416508928 | bytes 7471104 | tf_op jit(solution)/shard_map/tf,td->fd/dot_general | solution.py:550
  113.7 8.1 %norm_two.1 = (bf16[1024,768]{1,0:T(8,128)(2,1)}, bf16[384,1024]{1,0:T(8,128)(2,1)}, bf16[384,1024]{1,0:T(8,128)(2,1)}, f32[8,768]{1,0:T(8,128)}) custom-call(s32[1]{0:T(128)} %bitcast.half_ref.place_ref, bf16[1024,768]{1,0:T(8,128)(2,1)} %get-tuple-element.48.own_ref, bf16[1024,768]{1,0:T(8,128)(2,1)} %collective-permute-done.9.other_ref, ...), custom_call_target="tpu_custom_call" | custom-call | tf_op jit(solution)/shard_map/norm_two/pallas_call | solution.py:412
  123.5 6.7 %convolution_convert_fusion.1 = bf16[768,768]{1,0:T(8,128)(2,1)} fusion(bf16[2048,768]{1,0:T(8,128)(2,1)} %get-tuple-element.61, bf16[2048,768]{1,0:T(8,128)(2,1)} %get-tuple-element.62), kind=kOutput, calls=%fused_computation.4 | convolution fusion | flops 2416508928 | bytes 7471104 | tf_op jit(solution)/shard_map/td,tf->df/dot_general | solution.py:551
  130.9 10.7 %collective-permute-done.10 = bf16[384,1024]{1,0:T(8,128)(2,1)S(1)} collective-permute-done((bf16[384,1024]{1,0:T(8,128)(2,1)}, bf16[384,1024]{1,0:T(8,128)(2,1)S(1)}, u32[]{:S(2)}, u32[]{:S(2)}) %collective-permute-start.10) | collective-permute-done | bytes 786464 | tf_op jit(solution)/shard_map/ppermute | solution.py:485
  148.1 22.4 %attend_back.1 = (bf16[2048,192]{1,0:T(8,128)(2,1)}, bf16[2048,192]{1,0:T(8,128)(2,1)}, bf16[2048,192]{1,0:T(8,128)(2,1)}) custom-call(s32[1]{0:T(128)} %bitcast.half_ref.place_ref, s32[8]{0:T(128)} %get-tuple-element.37.info_ref, bf16[3,2048,128]{2,1,0:T(8,128)(2,1)} %get-tuple-element.38.q_ref, bf16[3,2048,128]{2,1,0:T(8,128)(2,1)} %get-tuple-element.39.k_ref, ...), custom_call_target="tpu_custom_call" | custom-call | tf_op jit(solution)/shard_map/attend_back/pallas_call | solution.py:306
  170.4 5.1 %first_grad.3 = bf16[1024,768]{1,0:T(8,128)(2,1)} custom-call(s32[1]{0:T(128)S(6)} %sub.7.half_ref.place_ref, bf16[2048,192]{1,0:T(8,128)(2,1)} %get-tuple-element.53.dq_ref, bf16[2048,192]{1,0:T(8,128)(2,1)} %get-tuple-element.54.dk_ref, bf16[2048,192]{1,0:T(8,128)(2,1)} %get-tuple-element.55.dv_ref, bf16[3,768,192]{2,1,0:T(8,128)(2,1)} %copy.25.w_ref), custom_call_target="tpu_custom_call" | custom-call | tf_op jit(solution)/shard_map/first_grad/pallas_call | solution.py:442
  175.6 2.4 add_convert_fusion.2
  184.9 5.1 %first_grad.2.own_ref = bf16[1024,768]{1,0:T(8,128)(2,1)} custom-call(s32[1]{0:T(128)} %bitcast.half_ref.place_ref, bf16[2048,192]{1,0:T(8,128)(2,1)} %get-tuple-element.53.dq_ref, bf16[2048,192]{1,0:T(8,128)(2,1)} %get-tuple-element.54.dk_ref, bf16[2048,192]{1,0:T(8,128)(2,1)} %get-tuple-element.55.dv_ref, bf16[3,768,192]{2,1,0:T(8,128)(2,1)} %copy.25.w_ref), custom_call_target="tpu_custom_call" | custom-call | tf_op jit(solution)/shard_map/first_grad/pallas_call | solution.py:442
  190.1 5.8 %norm_one.1 = (bf16[1024,768]{1,0:T(8,128)(2,1)}, f32[8,768]{1,0:T(8,128)}) custom-call(s32[1]{0:T(128)} %bitcast.half_ref.place_ref, bf16[1024,768]{1,0:T(8,128)(2,1)} %first_grad.2.own_ref, bf16[1024,768]{1,0:T(8,128)(2,1)} %collective-permute-done.12.other_ref, bf16[2048,768]{1,0:T(8,128)(2,1)} %x_ref.7, bf16[1024,768]{1,0:T(8,128)(2,1)} %get-tuple-element.56.gm_ref, ...), custom_call_target="tpu_custom_call" | custom-call | tf_op jit(solution)/shard_map/norm_one/pallas_call | solution.py:471
  197.6 17.9 %collective-permute-done.7 = bf16[1024,768]{1,0:T(8,128)(2,1)} collective-permute-done((bf16[1024,768]{1,0:T(8,128)(2,1)S(1)}, bf16[1024,768]{1,0:T(8,128)(2,1)}, u32[]{:S(2)}, u32[]{:S(2)}) %collective-permute-start.7) | collective-permute-done | bytes 1572896 | tf_op jit(solution)/shard_map/ppermute | solution.py:485
  215.7 3.0 constant_dynamic-update-slice_fusion.3
  218.7 29.9 %collective-permute-done.13 = bf16[1024,768]{1,0:T(8,128)(2,1)S(1)} collective-permute-done((bf16[1024,768]{1,0:T(8,128)(2,1)}, bf16[1024,768]{1,0:T(8,128)(2,1)S(1)}, u32[]{:S(2)}, u32[]{:S(2)}) %collective-permute-start.13) | collective-permute-done | bytes 1572896 | tf_op jit(solution)/shard_map/ppermute | solution.py:485
  251.9 78.5 %psum.35 = f32[4,768]{1,0:T(4,128)S(1)} all-reduce(f32[4,768]{1,0:T(4,128)S(1)} %pad_maximum_fusion.1), channel_id=1, replica_groups=mesh['dp'=8,'tensor'=4] {'dp','tensor'}, use_global_device_ids=true, to_apply=%region_0.1 | all-reduce | flops 3072 | bytes 24576 | tf_op jit(solution)/shard_map/psum | solution.py:566
  331.1 2.7 constant_dynamic-update-slice_fusion.2
  333.8 28.1 %all-reduce.3.cloned.1.call-done = (bf16[3,768,192]{1,2,0:T(8,128)(2,1)}, bf16[192,768]{1,0:T(8,128)(2,1)}, bf16[768,768]{1,0:T(8,128)(2,1)}, bf16[768,768]{1,0:T(8,128)(2,1)}) async-done(((bf16[3,768,192]{1,2,0:T(8,128)(2,1)}, bf16[192,768]{1,0:T(8,128)(2,1)}, bf16[768,768]{1,0:T(8,128)(2,1)}, bf16[768,768]{1,0:T(8,128)(2,1)}), (bf16[3,768,192]{1,2,0:T(8,128)(2,1)}, bf16[192,768]{1,0:T(8,128)(2,1)}, ...) | async-done | bytes 3538960 | tf_op jit(solution)/shard_map/psum | solution.py:564
  361.9 2.9 convert_element_type.126
  (108 shorter events, 37.3 us)
Async XLA Ops:
  7.2 354.7 %all-reduce.3.cloned.1.call-start = ((), (), s32[]{:S(2)}) async-start(), calls=%async_computation | async-start | bytes 7077888 | tf_op jit(solution)/shard_map/psum | solution.py:564
  23.1 42.7 %copy-start.14 = (bf16[192,768]{1,0:T(8,128)(2,1)S(1)}, bf16[192,768]{1,0:T(8,128)(2,1)}, u32[]{:S(2)}) copy-start(bf16[192,768]{1,0:T(8,128)(2,1)} %w0.5) | copy-start | bytes 884740
  23.1 52.1 %copy-start.23 = (f32[768]{0:T(1024)S(1)}, f32[768]{0:T(1024)}, u32[]{:S(2)}) copy-start(f32[768]{0:T(1024)} %param.19) | copy-start | bytes 9220
  23.1 52.8 %copy-start.24 = (f32[768]{0:T(1024)S(1)}, f32[768]{0:T(1024)}, u32[]{:S(2)}) copy-start(f32[768]{0:T(1024)} %param.20) | copy-start | bytes 9220
  45.1 20.7 %collective-permute-start.1 = (bf16[192,2048]{1,0:T(8,128)(2,1)}, bf16[192,2048]{1,0:T(8,128)(2,1)S(1)}, u32[]{:S(2)}, u32[]{:S(2)}) collective-permute-start(bf16[192,2048]{1,0:T(8,128)(2,1)} %get-tuple-element.41.a0.att_ref), channel_id=1, source_target_pairs={{0,2},{1,3},{2,0},{3,1},{4,6},{5,7},{6,4},{7,5},{8,10},{9,11},{10,... | collective-permute-start | bytes 2359304 | tf_op jit(solution)/shard_map/ppermute | solution.py:485
  48.1 28.9 %collective-permute-start = (bf16[192,2048]{1,0:T(8,128)(2,1)}, bf16[192,2048]{1,0:T(8,128)(2,1)S(1)}, u32[]{:S(2)}, u32[]{:S(2)}) collective-permute-start(bf16[192,2048]{1,0:T(8,128)(2,1)} %get-tuple-element.41.a0.att_ref), channel_id=1, source_target_pairs={{0,1},{1,0},{2,3},{3,2},{4,5},{5,4},{6,7},{7,6},{8,9},{9,8},{10,11... | collective-permute-start | bytes 2359304 | tf_op jit(solution)/shard_map/ppermute | solution.py:485
  65.8 11.2 %collective-permute-start.2 = (bf16[192,2048]{1,0:T(8,128)(2,1)S(1)}, bf16[192,2048]{1,0:T(8,128)(2,1)S(1)}, u32[]{:S(2)}, u32[]{:S(2)}) collective-permute-start(bf16[192,2048]{1,0:T(8,128)(2,1)S(1)} %collective-permute-done.1.a2), channel_id=1, source_target_pairs={{0,1},{1,0},{2,3},{3,2},{4,5},{5,4},{6,7},{7,6},{8,9},{9,8},{10,11... | collective-permute-start | bytes 2359304 | tf_op jit(solution)/shard_map/ppermute | solution.py:485
  65.8 9.4 %collective-permute-start.4 = (bf16[192,768]{1,0:T(8,128)(2,1)S(1)}, bf16[192,768]{1,0:T(8,128)(2,1)S(1)}, u32[]{:S(2)}, u32[]{:S(2)}) collective-permute-start(bf16[192,768]{1,0:T(8,128)(2,1)S(1)} %copy-done.14), channel_id=1, source_target_pairs={{0,2},{1,3},{2,0},{3,1},{4,6},{5,7},{6,4},{7,5},{8,10},{9,11},{10,... | collective-permute-start | bytes 884744 | tf_op jit(solution)/shard_map/ppermute | solution.py:485
  67.6 8.8 %collective-permute-start.3 = (bf16[192,768]{1,0:T(8,128)(2,1)S(1)}, bf16[192,768]{1,0:T(8,128)(2,1)S(1)}, u32[]{:S(2)}, u32[]{:S(2)}) collective-permute-start(bf16[192,768]{1,0:T(8,128)(2,1)S(1)} %copy-done.14), channel_id=1, source_target_pairs={{0,1},{1,0},{2,3},{3,2},{4,5},{5,4},{6,7},{7,6},{8,9},{9,8},{10,11... | collective-permute-start | bytes 884744 | tf_op jit(solution)/shard_map/ppermute | solution.py:485
  75.2 1.7 collective-permute-start.5
  93.1 20.6 %collective-permute-start.9 = (bf16[1024,768]{1,0:T(8,128)(2,1)}, bf16[1024,768]{1,0:T(8,128)(2,1)}, u32[]{:S(2)}, u32[]{:S(2)}) collective-permute-start(bf16[1024,768]{1,0:T(8,128)(2,1)} %get-tuple-element.49), channel_id=1, source_target_pairs={{0,1},{1,0},{2,3},{3,2},{4,5},{5,4},{6,7},{7,6},{8,9},{9,8},{10,11... | collective-permute-start | bytes 4718600 | tf_op jit(solution)/shard_map/ppermute | solution.py:485
  93.3 82.3 %collective-permute-start.6 = (bf16[1024,768]{1,0:T(8,128)(2,1)}, bf16[1024,768]{1,0:T(8,128)(2,1)}, u32[]{:S(2)}, u32[]{:S(2)}) collective-permute-start(bf16[1024,768]{1,0:T(8,128)(2,1)} %get-tuple-element.46), channel_id=1, source_target_pairs={{0,1},{1,0},{2,3},{3,2},{4,5},{5,4},{6,7},{7,6},{8,9},{9,8},{10,11... | collective-permute-start | bytes 4718600 | tf_op jit(solution)/shard_map/ppermute | solution.py:485
  121.8 19.8 %collective-permute-start.10 = (bf16[384,1024]{1,0:T(8,128)(2,1)}, bf16[384,1024]{1,0:T(8,128)(2,1)S(1)}, u32[]{:S(2)}, u32[]{:S(2)}) collective-permute-start(bf16[384,1024]{1,0:T(8,128)(2,1)} %get-tuple-element.52), channel_id=1, source_target_pairs={{0,2},{1,3},{2,0},{3,1},{4,6},{5,7},{6,4},{7,5},{8,10},{9,11},{10,... | collective-permute-start | bytes 2359304 | tf_op jit(solution)/shard_map/ppermute | solution.py:485
  130.8 13.6 %collective-permute-start.16 = (bf16[192,768]{1,0:T(8,128)(2,1)S(1)}, bf16[192,768]{1,0:T(8,128)(2,1)S(1)}, u32[]{:S(2)}, u32[]{:S(2)}) collective-permute-start(bf16[192,768]{1,0:T(8,128)(2,1)S(1)} %convolution_convert_fusion.2), channel_id=1, source_target_pairs={{0,1},{1,0},{2,3},{3,2},{4,5},{5,4},{6,7},{7,6},{8,9},{9,8},{10,11... | collective-permute-start | bytes 884744 | tf_op jit(solution)/shard_map/ppermute | solution.py:485
  142.6 4.7 %collective-permute-start.11 = (bf16[192,1024]{1,0:T(8,128)(2,1)S(1)}, bf16[192,1024]{1,0:T(8,128)(2,1)S(1)}, u32[]{:S(2)}, u32[]{:S(2)}) collective-permute-start(bf16[192,1024]{1,0:T(8,128)(2,1)S(1)} %get-tuple-element.76), channel_id=1, source_target_pairs={{0,1},{1,0},{2,3},{3,2},{4,5},{5,4},{6,7},{7,6},{8,9},{9,8},{10,11... | collective-permute-start | bytes 1179656 | tf_op jit(solution)/shard_map/ppermute | solution.py:485
  143.9 34.5 %collective-permute-start.15 = (bf16[192,768]{1,0:T(8,128)(2,1)}, bf16[192,768]{1,0:T(8,128)(2,1)S(1)}, u32[]{:S(2)}, u32[]{:S(2)}) collective-permute-start(bf16[192,768]{1,0:T(8,128)(2,1)} %convolution_convert_fusion.4), channel_id=1, source_target_pairs={{0,1},{1,0},{2,3},{3,2},{4,5},{5,4},{6,7},{7,6},{8,9},{9,8},{10,11... | collective-permute-start | bytes 884744 | tf_op jit(solution)/shard_map/ppermute | solution.py:485
  145.6 32.8 %collective-permute-start.17 = (bf16[192,768]{1,0:T(8,128)(2,1)}, bf16[192,768]{1,0:T(8,128)(2,1)}, u32[]{:S(2)}, u32[]{:S(2)}) collective-permute-start(bf16[192,768]{1,0:T(8,128)(2,1)} %fusion.5), channel_id=1, source_target_pairs={{0,2},{1,3},{2,0},{3,1},{4,6},{5,7},{6,4},{7,5},{8,10},{9,11},{10,... | collective-permute-start | bytes 884744 | tf_op jit(solution)/shard_map/ppermute | solution.py:485
  175.6 14.5 %collective-permute-start.12 = (bf16[1024,768]{1,0:T(8,128)(2,1)}, bf16[1024,768]{1,0:T(8,128)(2,1)}, u32[]{:S(2)}, u32[]{:S(2)}) collective-permute-start(bf16[1024,768]{1,0:T(8,128)(2,1)} %first_grad.3), channel_id=1, source_target_pairs={{0,1},{1,0},{2,3},{3,2},{4,5},{5,4},{6,7},{7,6},{8,9},{9,8},{10,11... | collective-permute-start | bytes 4718600 | tf_op jit(solution)/shard_map/ppermute | solution.py:485
  178.0 37.4 %collective-permute-start.7 = (bf16[1024,768]{1,0:T(8,128)(2,1)S(1)}, bf16[1024,768]{1,0:T(8,128)(2,1)}, u32[]{:S(2)}, u32[]{:S(2)}) collective-permute-start(bf16[1024,768]{1,0:T(8,128)(2,1)S(1)} %add_convert_fusion.2), channel_id=1, source_target_pairs={{0,2},{1,3},{2,0},{3,1},{4,6},{5,7},{6,4},{7,5},{8,10},{9,11},{10,... | collective-permute-start | bytes 4718600 | tf_op jit(solution)/shard_map/ppermute | solution.py:485
  195.8 52.7 %collective-permute-start.13 = (bf16[1024,768]{1,0:T(8,128)(2,1)}, bf16[1024,768]{1,0:T(8,128)(2,1)S(1)}, u32[]{:S(2)}, u32[]{:S(2)}) collective-permute-start(bf16[1024,768]{1,0:T(8,128)(2,1)} %get-tuple-element.57), channel_id=1, source_target_pairs={{0,2},{1,3},{2,0},{3,1},{4,6},{5,7},{6,4},{7,5},{8,10},{9,11},{10,... | collective-permute-start | bytes 4718600 | tf_op jit(solution)/shard_map/ppermute | solution.py:485
  218.7 31.8 %copy-start.13 = (bf16[2048,768]{1,0:T(8,128)(2,1)}, bf16[2048,768]{1,0:T(8,128)(2,1)S(1)}, u32[]{:S(2)}) copy-start(bf16[2048,768]{1,0:T(8,128)(2,1)S(1)} %get-tuple-element.74) | copy-start | bytes 9437188
  218.7 30.1 %copy-start.17 = (bf16[1024,768]{1,0:T(8,128)(2,1)S(1)}, bf16[1024,768]{1,0:T(8,128)(2,1)}, u32[]{:S(2)}) copy-start(bf16[1024,768]{1,0:T(8,128)(2,1)} %get-tuple-element.57) | copy-start | bytes 4718596
  218.7 112.4 %collective-permute-start.8 = (bf16[1024,768]{1,0:T(8,128)(2,1)}, bf16[1024,768]{1,0:T(8,128)(2,1)}, u32[]{:S(2)}, u32[]{:S(2)}) collective-permute-start(bf16[1024,768]{1,0:T(8,128)(2,1)} %get-tuple-element.75), channel_id=1, source_target_pairs={{0,1},{1,0},{2,3},{3,2},{4,5},{5,4},{6,7},{7,6},{8,9},{9,8},{10,11... | collective-permute-start | bytes 4718600 | tf_op jit(solution)/shard_map/ppermute | solution.py:485
  250.4 118.2 %collective-permute-start.14 = (bf16[1024,768]{1,0:T(8,128)(2,1)}, bf16[1024,768]{1,0:T(8,128)(2,1)}, u32[]{:S(2)}, u32[]{:S(2)}) collective-permute-start(bf16[1024,768]{1,0:T(8,128)(2,1)} %get-tuple-element.73), channel_id=1, source_target_pairs={{0,1},{1,0},{2,3},{3,2},{4,5},{5,4},{6,7},{7,6},{8,9},{9,8},{10,11... | collective-permute-start | bytes 4718600 | tf_op jit(solution)/shard_map/ppermute | solution.py:485
  (21 other events, 103.3 us)
Sparse Core Ops, SparseCore 0:
  185.0 176.8 all-reduce.2

commit v2 on v1

v2 whole, which is shorter than its diff:
```python
from functools import partial

import jax
import jax.numpy as jnp
from jax import lax
from jax.experimental import pallas as pl
from jax.experimental.pallas import tpu as pltpu
from jax.sharding import PartitionSpec as P

HD = 64
LANES = 128
BLK = 256
BIG = 1e30
ZERO, MINE, THEIRS = 3, 4, 5
F32 = jnp.float32
BF16 = jnp.bfloat16
VMEM = pltpu.VMEM
SMEM = pltpu.SMEM
NN = (((1,), (0,)), ((), ()))
NT = (((1,), (1,)), ((), ()))
TN = (((0,), (0,)), ((), ()))


def mm(a, b, dims=NN):
    return lax.dot_general(a, b, dims, preferred_element_type=F32)


def normalized(values):
    average = jnp.mean(values, -1, keepdims=True)
    centred = values - average
    spread = jnp.mean(centred * centred, -1, keepdims=True)
    scale = lax.rsqrt(spread + 1e-05)
    return centred * scale, scale


def norm_back(e, n, scale):
    return (e - jnp.mean(e, -1, keepdims=True) - n * jnp.mean(e * n, -1, keepdims=True)) * scale


def cost(us):
    return pl.CostEstimate(flops=int(us), bytes_accessed=int(us), transcendentals=0)


def front_kernel(live_ref, ids_ref, x_ref, norm_ref, w_ref,
                 first_ref, q_ref, k_ref, v_ref, info_ref, wp_ref):
    step = pl.program_id(0)

    @pl.when(step == 0)
    def _():
        ids = ids_ref[...]
        info_ref[0] = 0
        for s in range(1, 4):
            info_ref[s] = jnp.sum(jnp.where(ids < s, 1.0, 0.0)).astype(jnp.int32)
        info_ref[4] = ids.shape[1]
        info_ref[5] = live_ref[0]
        width = w_ref.shape[1]
        for c in range(3):
            wp_ref[c, 0:width, :] = w_ref[c]
            wp_ref[c, width:, :] = jnp.zeros_like(wp_ref[c, width:, :])

    n, _ = normalized(x_ref[...].astype(F32))
    first = (n * norm_ref[0:1, :] + norm_ref[1:2, :]).astype(BF16)
    first_ref[...] = first
    rows = step * BLK + lax.broadcasted_iota(jnp.int32, (BLK, LANES), 0)
    lane = lax.broadcasted_iota(jnp.int32, (BLK, LANES), 1)
    low = jnp.zeros((BLK, LANES), jnp.int32)
    high = jnp.zeros((BLK, LANES), jnp.int32)
    for s in range(4):
        low = jnp.where(lane == HD + s, info_ref[s], low)
        high = jnp.where(lane == HD + s, info_ref[s + 1], high)
    inside = (rows >= low) & (rows < high)
    flag = lane == HD + 4
    in_ids = (lane >= HD) & (lane < HD + 4)
    q_ext = jnp.where(flag | (in_ids & ~inside), -BIG, 0.0)
    k_ext = jnp.where((in_ids & inside) | (flag & (rows >= info_ref[5])), 1.0, 0.0)
    v_ext = jnp.zeros((BLK, LANES), F32)
    own = lane < HD
    for c, (ref, ext) in enumerate(((q_ref, q_ext), (k_ref, k_ext), (v_ref, v_ext))):
        res = mm(first, wp_ref[c], NT)
        if c == 0:
            res = res * 0.125
        pair = res[:, 0:LANES]
        for h, part in enumerate((pair, pltpu.roll(pair, HD, 1), res[:, LANES:2 * LANES])):
            ref[h] = jnp.where(own, part, ext).astype(BF16)


def front(live, ids, tokens, norms, weight):
    length, dim = tokens.shape
    count = length // BLK
    heads = weight.shape[1] // HD
    full = lambda *shape: pl.BlockSpec(shape, lambda i: (0,) * len(shape))
    head_spec = pl.BlockSpec((heads, BLK, LANES), lambda i: (0, i, 0))
    head_shape = jax.ShapeDtypeStruct((heads, length, LANES), BF16)
    return pl.pallas_call(
        front_kernel,
        grid=(count,),
        in_specs=[
            pl.BlockSpec(memory_space=SMEM),
            full(1, length),
            pl.BlockSpec((BLK, dim), lambda i: (i, 0)),
            full(*norms.shape),
            full(*weight.shape),
        ],
        out_specs=[
            pl.BlockSpec((BLK, dim), lambda i: (i, 0)),
            head_spec, head_spec, head_spec,
            pl.BlockSpec(memory_space=SMEM),
        ],
        out_shape=[
            jax.ShapeDtypeStruct((length, dim), BF16),
            head_shape, head_shape, head_shape,
            jax.ShapeDtypeStruct((8,), jnp.int32),
        ],
        scratch_shapes=[VMEM((3, 2 * LANES, dim), BF16)],
        cost_estimate=cost(10),
        name="front",
    )(live, ids, tokens, norms, weight)


def segment_span(info_ref, first, last):
    low, high = jnp.int32(0), info_ref[4]
    for s in range(3, 0, -1):
        at = info_ref[s]
        high = jnp.where(at > last, at, high)
    for s in range(1, 4):
        at = info_ref[s]
        low = jnp.where(at <= first, at, low)
    return low, high


def diagonal_mask(scores, base, live):
    key = lax.broadcasted_iota(jnp.int32, scores.shape, 0)
    query = lax.broadcasted_iota(jnp.int32, scores.shape, 1)
    return jnp.where((key + base >= live) & (key != query), -BIG, scores)


def drop_flag(block):
    lane = lax.broadcasted_iota(jnp.int32, block.shape, 1)
    return jnp.where(lane == HD + 4, 0.0, block.astype(F32)).astype(BF16)


def tile_rows(tile):
    return pl.ds(pl.multiple_of(tile * BLK, BLK), BLK)


def attend_kernel(info_ref, q_ref, k_ref, v_ref, att_ref, lse_ref, vt_ref, acc_ref, max_ref, s_ref):
    step = pl.program_id(0)
    heads, count = vt_ref.shape[0], vt_ref.shape[1]
    extra = vt_ref.shape[2] - HD

    @pl.when(step == 0)
    def _():
        one = jnp.where(lax.broadcasted_iota(jnp.int32, (extra, BLK), 0) == 0, 1.0, 0.0).astype(BF16)
        def fill(kb, _):
            for h in range(heads):
                turned = jnp.transpose(v_ref[h, tile_rows(kb), :].astype(F32))
                vt_ref[h, kb, 0:HD, :] = turned[0:HD].astype(BF16)
                vt_ref[h, kb, HD:HD + extra, :] = one
            return 0
        lax.fori_loop(0, count, fill, 0)
    base = step * BLK
    live = info_ref[5]
    low, high = segment_span(info_ref, base, base + BLK - 1)
    begin = low // BLK
    end = (jnp.minimum(high, live) + (BLK - 1)) // BLK
    total = jnp.maximum(end - begin, 0)
    total = total - jnp.where((begin <= step) & (step < end), 1, 0)
    at = lambda t: begin + t + jnp.where(begin + t >= step, 1, 0)
    part = lambda x: jnp.max(x.reshape(BLK // 8, 8, BLK), 0)
    odd = total % 2 == 1
    skip = jnp.where(odd, 1, 0)

    def score(h, kb):
        a = mm(k_ref[h, tile_rows(kb), :], q_ref[h], NT)
        s_ref[h, kb] = a
        return part(a)

    def diag(h):
        a = diagonal_mask(mm(k_ref[h, tile_rows(step), :], drop_flag(q_ref[h]), NT), base, live)
        s_ref[h, step] = a
        return part(a)

    @pl.when(odd)
    def _():
        for h in range(heads):
            max_ref[h] = jnp.maximum(diag(h), score(h, at(0)))

    @pl.when(~odd)
    def _():
        for h in range(heads):
            max_ref[h] = diag(h)

    def one(t, _):
        ka, kb = at(skip + 2 * t), at(skip + 2 * t + 1)
        for h in range(heads):
            max_ref[h] = jnp.maximum(max_ref[h], jnp.maximum(score(h, ka), score(h, kb)))
        return 0
    lax.fori_loop(0, (total - skip) // 2, one, 0)
    for h in range(heads):
        max_ref[h] = jnp.broadcast_to(jnp.max(max_ref[h], 0, keepdims=True), (8, BLK))
    pv = lambda h, kb: mm(vt_ref[h, kb], jnp.exp(s_ref[h, kb] - max_ref[h, 0:1]).astype(BF16))

    @pl.when(odd)
    def _():
        for h in range(heads):
            acc_ref[h] = pv(h, step) + pv(h, at(0))

    @pl.when(~odd)
    def _():
        for h in range(heads):
            acc_ref[h] = pv(h, step)

    def two(t, _):
        ka, kb = at(skip + 2 * t), at(skip + 2 * t + 1)
        for h in range(heads):
            acc_ref[h] += pv(h, ka) + pv(h, kb)
        return 0
    lax.fori_loop(0, (total - skip) // 2, two, 0)
    for h in range(heads):
        sums = acc_ref[h, HD:HD + 1, :]
        att_ref[h * HD:(h + 1) * HD, :] = (acc_ref[h, 0:HD, :] / sums).astype(BF16)
        lse_ref[0, h:h + 1, :] = max_ref[h, 0:1] + jnp.log(sums)


def attend(info, q, k, v):
    heads, length, _ = q.shape
    count = length // BLK
    whole = pl.BlockSpec((heads, length, LANES), lambda i: (0, 0, 0))
    return pl.pallas_call(
        attend_kernel,
        grid=(count,),
        in_specs=[
            pl.BlockSpec(memory_space=SMEM),
            pl.BlockSpec((heads, BLK, LANES), lambda i: (0, i, 0)),
            whole, whole,
        ],
        out_specs=[
            pl.BlockSpec((heads * HD, BLK), lambda i: (0, i)),
            pl.BlockSpec((1, 8, BLK), lambda i: (i, 0, 0)),
        ],
        out_shape=[
            jax.ShapeDtypeStruct((heads * HD, length), BF16),
            jax.ShapeDtypeStruct((count, 8, BLK), F32),
        ],
        scratch_shapes=[
            VMEM((heads, count, HD + 16, BLK), BF16),
            VMEM((heads, HD + 16, BLK), F32),
            VMEM((heads, 8, BLK), F32),
            VMEM((heads, count, BLK, BLK), F32),
        ],
        cost_estimate=cost(20),
        name="attend",
    )(info, q, k, v)


def attend_back_kernel(half_ref, info_ref, q_ref, k_ref, v_ref, att_ref, lse_ref, own_ref, other_ref,
                       dq_ref, dk_ref, dv_ref, dot_ref, do_ref, delta_ref, dqt_ref, kt_ref, dkv_ref,
                       p_ref, g_ref):
    step = pl.program_id(0)
    heads, count = dqt_ref.shape[0], dqt_ref.shape[1]
    half = count // 2

    @pl.when(step == 0)
    def _():
        def fill(t, _):
            for place, ref in ((half_ref[MINE], own_ref), (1 - half_ref[MINE], other_ref)):
                qb = place * half + t
                for h in range(heads):
                    cols = pl.ds(pl.multiple_of(t * BLK, BLK), BLK)
                    part = ref[h * HD:(h + 1) * HD, cols].astype(F32)
                    at = pl.ds(pl.multiple_of(qb * BLK, BLK), BLK)
                    att = att_ref[h * HD:(h + 1) * HD, at].astype(F32)
                    delta_ref[qb, h:h + 1, :] = jnp.sum(part * att, 0, keepdims=True)
                    padded = jnp.concatenate([part, jnp.zeros_like(part)], 0)
                    dot_ref[h, qb] = padded.astype(BF16)
                    do_ref[h, qb] = jnp.transpose(padded).astype(BF16)
                    dqt_ref[h, qb] = jnp.zeros_like(dqt_ref[h, qb])
            return 0
        lax.fori_loop(0, half, fill, 0)

    base = step * BLK
    live = info_ref[5]
    low, high = segment_span(info_ref, base, base + BLK - 1)
    for h in range(heads):
        kt_ref[h] = jnp.transpose(k_ref[h].astype(F32))[0:HD].astype(BF16)
        dkv_ref[0, h] = jnp.zeros_like(dkv_ref[0, h])
        dkv_ref[1, h] = jnp.zeros_like(dkv_ref[1, h])

    def produce(qb, diagonal):
        for h in range(heads):
            q = q_ref[h, tile_rows(qb), :]
            if diagonal:
                scores = diagonal_mask(mm(k_ref[h], drop_flag(q), NT), base, live)
            else:
                scores = mm(k_ref[h], q, NT)
            probs = jnp.exp(scores - lse_ref[qb, h:h + 1, :])
            p_ref[h] = probs.astype(BF16)
            g_ref[h] = (probs * (mm(v_ref[h], dot_ref[h, qb]) - delta_ref[qb, h:h + 1, :])).astype(BF16)

    def consume(qb):
        for h in range(heads):
            dkv_ref[1, h] += mm(p_ref[h], do_ref[h, qb])
            dkv_ref[0, h] += mm(g_ref[h], q_ref[h, tile_rows(qb), :])
            dqt_ref[h, qb] += mm(kt_ref[h], g_ref[h])

    begin = low // BLK
    end = (high + (BLK - 1)) // BLK
    total = jnp.where(base < live, end - begin - 1, 0)
    produce(step, True)

    def body(t, last):
        consume(last)
        qb = begin + t
        qb = qb + jnp.where(qb >= step, 1, 0)
        produce(qb, False)
        return qb

    consume(lax.fori_loop(0, total, body, step))
    lane = lax.broadcasted_iota(jnp.int32, (BLK, LANES), 1)
    for c, ref in enumerate((dk_ref, dv_ref)):
        two = jnp.where(lane < HD, dkv_ref[c, 0], pltpu.roll(dkv_ref[c, 1], HD, 1))
        ref[:, 0:LANES] = two.astype(BF16)
        ref[:, LANES:LANES + HD] = dkv_ref[c, 2][:, 0:HD].astype(BF16)

    @pl.when(step == count - 1)
    def _():
        def drain(qb, _):
            rows = pl.ds(pl.multiple_of(qb * BLK, BLK), BLK)
            two = jnp.concatenate([dqt_ref[0, qb], dqt_ref[1, qb]], 0)
            dq_ref[rows, 0:LANES] = (jnp.transpose(two) * 0.125).astype(BF16)
            last = jnp.concatenate([dqt_ref[2, qb], dqt_ref[2, qb]], 0)
            dq_ref[rows, LANES:LANES + HD] = (jnp.transpose(last) * 0.125)[:, 0:HD].astype(BF16)
            return 0
        lax.fori_loop(0, count, drain, 0)


def attend_back(half, info, q, k, v, att, lse, own, other):
    heads, length, _ = q.shape
    count = length // BLK
    width = heads * HD
    whole = pl.BlockSpec((heads, length, LANES), lambda i: (0, 0, 0))
    block = pl.BlockSpec((heads, BLK, LANES), lambda i: (0, i, 0))
    part = jax.ShapeDtypeStruct((length, width), BF16)
    return pl.pallas_call(
        attend_back_kernel,
        grid=(count,),
        in_specs=[
            pl.BlockSpec(memory_space=SMEM),
            pl.BlockSpec(memory_space=SMEM),
            whole, block, block,
            pl.BlockSpec((width, length), lambda i: (0, 0)),
            pl.BlockSpec((count, 8, BLK), lambda i: (0, 0, 0)),
            pl.BlockSpec((width, length // 2), lambda i: (0, 0)),
            pl.BlockSpec((width, length // 2), lambda i: (0, 0)),
        ],
        out_specs=[
            pl.BlockSpec((length, width), lambda i: (0, 0)),
            pl.BlockSpec((BLK, width), lambda i: (i, 0)),
            pl.BlockSpec((BLK, width), lambda i: (i, 0)),
        ],
        out_shape=[part, part, part],
        scratch_shapes=[
            VMEM((heads, count, LANES, BLK), BF16),
            VMEM((heads, count, BLK, LANES), BF16),
            VMEM((count, 8, BLK), F32),
            VMEM((heads, count, HD, BLK), F32),
            VMEM((heads, HD, BLK), BF16),
            VMEM((2, heads, BLK, LANES), F32),
            VMEM((heads, BLK, BLK), BF16),
            VMEM((heads, BLK, BLK), BF16),
        ],
        cost_estimate=cost(28),
        name="attend_back",
    )(half, info, q, k, v, att, lse, own, other)


def middle_kernel(half_ref, a0, a1, a2, a3, w0, w1, w2, w3, x_ref, go_ref, norm_ref, up_ref, down_ref,
                  *refs):
    second_ref, hidden_ref, pre_ref, out_ref, gs_ref, mid_ref = refs[-6:]
    proj = mm(a0[...], w0[...], TN)
    for a, w in ((a1, w1), (a2, w2), (a3, w3)):
        proj = proj + mm(a[...], w[...], TN)
    middle = x_ref[...].astype(F32) + proj
    mid_ref[...] = middle
    n, _ = normalized(middle)
    second = (n * norm_ref[2:3, :] + norm_ref[3:4, :]).astype(BF16)
    second_ref[...] = second
    pre = mm(second, up_ref[...])
    phi = 0.5 + 0.5 * lax.erf(pre * 0.7071067811865476)
    hidden = (pre * phi).astype(BF16)
    hidden_ref[...] = hidden
    slope = phi + pre * (0.3989422804014327 * jnp.exp(-0.5 * pre * pre))
    grad_pre = (mm(go_ref[...], down_ref[...], NT) * slope).astype(BF16)
    pre_ref[...] = grad_pre
    out_ref[...] = (0.25 * middle + mm(hidden, down_ref[...])).astype(BF16)
    gs_ref[...] = mm(grad_pre, up_ref[...], NT).astype(BF16)


def middle_part(table, at, att, weights, tokens, grad_out, norms, up, down, carried):
    length, dim = tokens.shape
    width = att[0].shape[0]
    steps = length // BLK // 2
    rows = pl.BlockSpec((BLK, dim), lambda i, p: (p[at] * steps + i, 0))
    local = pl.BlockSpec((BLK, dim), lambda i, p: (i, 0))
    fixed = lambda *shape: pl.BlockSpec(shape, lambda i, p: (0,) * len(shape))
    anywhere = pl.BlockSpec(memory_space=pl.ANY)
    hidden_dim = up.shape[1]
    full = lambda d: jax.ShapeDtypeStruct((length, d), BF16)
    part = lambda t: jax.ShapeDtypeStruct((length // 2, dim), t)
    first_alias = 1 + 4 + 4 + 5
    return pl.pallas_call(
        middle_kernel,
        grid_spec=pltpu.PrefetchScalarGridSpec(
            num_scalar_prefetch=1,
            grid=(steps,),
            in_specs=[pl.BlockSpec((width, BLK), lambda i, p: (0, p[at] * steps + i))] * 4
            + [fixed(width, dim)] * 4
            + [rows, rows, fixed(*norms.shape), fixed(*up.shape), fixed(*down.shape)]
            + [anywhere] * len(carried),
            out_specs=[rows, rows, rows, local, local, local],
        ),
        out_shape=[full(dim), full(hidden_dim), full(hidden_dim), part(BF16), part(BF16), part(F32)],
        input_output_aliases={first_alias + i: i for i in range(len(carried))},
        cost_estimate=cost(14),
        name="middle",
    )(table, *att, *weights, tokens, grad_out, norms, up, down, *carried)


def norm_two_kernel(half_ref, own_ref, other_ref, mid_ref, go_ref, norm_ref, w0, w1, w2, w3,
                    gm_ref, keep_ref, send_ref, sums_ref):
    @pl.when(pl.program_id(0) == 0)
    def _():
        sums_ref[...] = jnp.zeros_like(sums_ref)
    g = own_ref[...].astype(F32) + other_ref[...].astype(F32)
    n, scale = normalized(mid_ref[...])
    sums_ref[0:1, :] += jnp.sum(g * n, 0, keepdims=True)
    sums_ref[1:2, :] += jnp.sum(g, 0, keepdims=True)
    gm = (0.5 * go_ref[...].astype(F32) + norm_back(g * norm_ref[2:3, :], n, scale)).astype(BF16)
    gm_ref[...] = gm
    width = w0.shape[0]
    keep_ref[0:width, :] = mm(w0[...], gm, NT).astype(BF16)
    keep_ref[width:2 * width, :] = mm(w1[...], gm, NT).astype(BF16)
    send_ref[0:width, :] = mm(w2[...], gm, NT).astype(BF16)
    send_ref[width:2 * width, :] = mm(w3[...], gm, NT).astype(BF16)


def norm_two(table, own, other, middle, grad_out, norms, weights):
    rows, dim = own.shape
    width = weights[0].shape[0]
    steps = rows // BLK
    local = pl.BlockSpec((BLK, dim), lambda i, p: (i, 0))
    fixed = lambda *shape: pl.BlockSpec(shape, lambda i, p: (0,) * len(shape))
    cols = pl.BlockSpec((2 * width, BLK), lambda i, p: (0, i))
    return pl.pallas_call(
        norm_two_kernel,
        grid_spec=pltpu.PrefetchScalarGridSpec(
            num_scalar_prefetch=1,
            grid=(steps,),
            in_specs=[local, local, local, pl.BlockSpec((BLK, dim), lambda i, p: (p[MINE] * steps + i, 0)),
                      fixed(*norms.shape)]
            + [fixed(width, dim)] * 4,
            out_specs=[local, cols, cols, fixed(8, dim)],
        ),
        out_shape=[
            jax.ShapeDtypeStruct((rows, dim), BF16),
            jax.ShapeDtypeStruct((2 * width, rows), BF16),
            jax.ShapeDtypeStruct((2 * width, rows), BF16),
            jax.ShapeDtypeStruct((8, dim), F32),
        ],
        cost_estimate=cost(8),
        name="norm_two",
    )(table, own, other, middle, grad_out, norms, *weights)


def first_total(dq_ref, dk_ref, dv_ref, w_ref):
    total = mm(dq_ref[...], w_ref[0])
    total = total + mm(dk_ref[...], w_ref[1])
    return total + mm(dv_ref[...], w_ref[2])


def first_grad_kernel(place_ref, dq_ref, dk_ref, dv_ref, w_ref, out_ref):
    out_ref[...] = first_total(dq_ref, dk_ref, dv_ref, w_ref).astype(BF16)


def first_grad(table, at, dq, dk, dv, weight):
    length, width = dq.shape
    dim = weight.shape[2]
    steps = length // BLK // 2
    rows = pl.BlockSpec((BLK, width), lambda i, p: (p[at] * steps + i, 0))
    return pl.pallas_call(
        first_grad_kernel,
        grid_spec=pltpu.PrefetchScalarGridSpec(
            num_scalar_prefetch=1,
            grid=(steps,),
            in_specs=[rows, rows, rows, pl.BlockSpec(weight.shape, lambda i, p: (0, 0, 0))],
            out_specs=pl.BlockSpec((BLK, dim), lambda i, p: (i, 0)),
        ),
        out_shape=jax.ShapeDtypeStruct((length // 2, dim), BF16),
        cost_estimate=cost(4),
        name="first_grad",
    )(table, dq, dk, dv, weight)


def norm_one_kernel(place_ref, dq_ref, dk_ref, dv_ref, w_ref, other_ref, x_ref, gm_ref, norm_ref, sums_two_ref,
                    out_ref, sums_ref):
    @pl.when(pl.program_id(0) == 0)
    def _():
        sums_ref[...] = sums_two_ref[...]
    g = first_total(dq_ref, dk_ref, dv_ref, w_ref) + other_ref[...].astype(F32)
    n, scale = normalized(x_ref[...].astype(F32))
    sums_ref[2:3, :] += jnp.sum(g * n, 0, keepdims=True)
    sums_ref[3:4, :] += jnp.sum(g, 0, keepdims=True)
    out_ref[...] = (gm_ref[...].astype(F32) + norm_back(g * norm_ref[0:1, :], n, scale)).astype(BF16)


def norm_one(table, dq, dk, dv, weight, other, tokens, gm, norms, sums_two):
    rows, dim = other.shape
    width = dq.shape[1]
    steps = rows // BLK
    local = pl.BlockSpec((BLK, dim), lambda i, p: (i, 0))
    placed = lambda d: pl.BlockSpec((BLK, d), lambda i, p: (p[MINE] * steps + i, 0))
    fixed = lambda *shape: pl.BlockSpec(shape, lambda i, p: (0,) * len(shape))
    return pl.pallas_call(
        norm_one_kernel,
        grid_spec=pltpu.PrefetchScalarGridSpec(
            num_scalar_prefetch=1,
            grid=(steps,),
            in_specs=[placed(width)] * 3 + [fixed(*weight.shape), local, placed(dim), local, fixed(*norms.shape),
                                            fixed(8, dim)],
            out_specs=[local, fixed(8, dim)],
        ),
        out_shape=[jax.ShapeDtypeStruct((rows, dim), BF16), jax.ShapeDtypeStruct((8, dim), F32)],
        cost_estimate=cost(10),
        name="norm_one",
    )(table, dq, dk, dv, weight, other, tokens, gm, norms, sums_two)


def fold_kernel(picks, cuts, table_ref, *refs):
    count = len(picks)
    ins, outs = refs[:2 * count], refs[2 * count:]
    for i in range(count):
        got, own = ins[2 * i], ins[2 * i + 1]
        base = table_ref[picks[i]] * got.shape[0]
        if cuts is None:
            at = pl.ds(pl.multiple_of(base, got.shape[0]), got.shape[0])
            outs[i][...] = (got[...].astype(F32) + own[at, :].astype(F32)).astype(BF16)
            continue
        keep, send = outs[2 * i], outs[2 * i + 1]
        rows = keep.shape[0]
        cut = table_ref[cuts[i]]
        for ref, half in ((keep, cut), (send, 1 - cut)):
            here = pl.ds(pl.multiple_of(half * rows, rows), rows)
            there = pl.ds(pl.multiple_of(base + half * rows, rows), rows)
            ref[...] = (got[here, :].astype(F32) + own[there, :].astype(F32)).astype(BF16)


def in_vmem(count):
    return [pl.BlockSpec(memory_space=VMEM)] * count


def fold(table, picks, cuts, pairs):
    outs, args = [], []
    for got, own in pairs:
        rows, dim = got.shape
        outs += [jax.ShapeDtypeStruct((rows, dim), BF16)] if cuts is None else [
            jax.ShapeDtypeStruct((rows // 2, dim), BF16)] * 2
        args += [got, own]
    res = pl.pallas_call(
        partial(fold_kernel, picks, cuts),
        in_specs=[pl.BlockSpec(memory_space=SMEM)] + in_vmem(len(args)),
        out_specs=in_vmem(len(outs)),
        out_shape=outs,
        cost_estimate=cost(1),
        name="fold",
    )(table, *args)
    return res if cuts is None else ([res[0], res[2]], [res[1], res[3]])


def join_kernel(bits, table_ref, *refs):
    count = len(bits)
    for i in range(count):
        own, got, out = refs[2 * i], refs[2 * i + 1], refs[2 * count + i]
        rows = own.shape[0]
        for ref, half in ((own, table_ref[bits[i]]), (got, 1 - table_ref[bits[i]])):
            out[pl.ds(pl.multiple_of(half * rows, rows), rows), :] = ref[...].astype(out.dtype)


def join(table, bits, pairs):
    outs, args = [], []
    for own, got in pairs:
        outs.append(jax.ShapeDtypeStruct((2 * own.shape[0], own.shape[1]), own.dtype))
        args += [own, got]
    return pl.pallas_call(
        partial(join_kernel, bits),
        in_specs=[pl.BlockSpec(memory_space=SMEM)] + in_vmem(len(args)),
        out_specs=in_vmem(len(outs)),
        out_shape=outs,
        cost_estimate=cost(1),
        name="join",
    )(table, *args)


def last_join_kernel(bits, table_ref, *refs):
    count = len(bits)
    for i in range(count):
        own, got, out = refs[2 * i], refs[2 * i + 1], refs[2 * count + i]
        for ref, half in ((own, table_ref[bits[i]]), (got, 1 - table_ref[bits[i]])):
            @pl.when(pl.program_id(0) == half)
            def _():
                out[...] = ref[...].astype(F32)


def last_join(table, bits, pairs):
    outs, specs, args = [], [], []
    for own, got in pairs:
        rows, dim = own.shape
        outs.append(jax.ShapeDtypeStruct((2 * rows, dim), F32))
        specs.append(pl.BlockSpec((rows, dim), lambda i: (i, 0)))
        args += [own, got]
    return pl.pallas_call(
        partial(last_join_kernel, bits),
        grid=(2,),
        in_specs=[pl.BlockSpec(memory_space=SMEM)] + in_vmem(len(args)),
        out_specs=specs,
        out_shape=outs,
        cost_estimate=cost(2),
        name="last_join",
    )(table, *args)


def dp_swap(value, distance):
    return lax.ppermute(value, "dp", [(d, d ^ distance) for d in range(lax.axis_size("dp"))])


ORDERS = ((0, 1, 2), (1, 2, 0))


def place_table():
    core = lax.axis_index("tensor") % 2
    code = lax.axis_index("dp") % 8 + 16 * core + 32 * (1 - core)
    return (code // jnp.array([1, 2, 4, 8, 16, 32, 64, 128], jnp.int32)) % 2


def dp_sum_pair(table, a, b, extra, held):
    if lax.axis_size("dp") != 8:
        a, b, extra = lax.psum((a, b, extra), "dp")
        return a.astype(F32), b.astype(F32), extra, held
    index = lax.axis_index("dp")
    rows = a.shape[0] // 2
    own = [a, b]
    send = [
        lax.dynamic_slice_in_dim(v, (1 - (index >> o[0]) % 2) * rows, rows, 0) for v, o in zip(own, ORDERS)
    ]
    for step in range(3):
        got = [dp_swap(v, 1 << o[step]) for v, o in zip(send, ORDERS)]
        extra = extra + dp_swap(extra, 1 << step)
        extra, got = lax.optimization_barrier((extra, got))
        picks = [o[0] if step == 0 else ZERO for o in ORDERS]
        pairs = list(zip(got, own))
        if step == 2:
            own = fold(table, picks, None, pairs)
            break
        own, send = fold(table, picks, [o[step + 1] for o in ORDERS], pairs)
    own, held = lax.optimization_barrier((own, held))
    for step in (2, 1, 0):
        got = [dp_swap(v, 1 << o[step]) for v, o in zip(own, ORDERS)]
        own = (join if step else last_join)(table, [o[step] for o in ORDERS], list(zip(own, got)))
    return *own, extra, held


def swap(value, distance):
    return lax.ppermute(value, "tensor", [(t, t ^ distance) for t in range(4)])


def add(a, b):
    return a.astype(F32) + b.astype(F32)


def both_halves(core, mine):
    other = swap(mine, 1)
    rows = mine.shape[0]
    full = jnp.zeros((2 * rows, mine.shape[1]), mine.dtype)
    full = lax.dynamic_update_slice(full, mine, (core * rows, 0))
    return lax.dynamic_update_slice(full, other, ((1 - core) * rows, 0))


def local(
    tokens,
    segment_ids,
    live_lengths,
    gain_one,
    shift_one,
    qkv_weight,
    out_weight,
    gain_two,
    shift_two,
    up_weight,
    down_weight,
    grad_out,
):
    core = lax.axis_index("tensor") % 2
    table = place_table()
    norms = jnp.stack([gain_one, shift_one, gain_two, shift_two])
    qkv = jnp.swapaxes(qkv_weight, 1, 2)
    w_far = swap(out_weight, 2)
    w_sib = swap(out_weight, 1)
    w_diag = swap(w_far, 1)

    first, q, k, v, info = front(live_lengths, segment_ids, tokens, norms, qkv)
    att, lse = attend(info, q, k, v)
    att, w_sib, w_far, w_diag = lax.optimization_barrier((att, w_sib, w_far, w_diag))
    weights = (out_weight, w_sib, w_far, w_diag)
    att_far = swap(att, 2)
    att_sib = swap(att, 1)
    att_diag = swap(att_far, 1)
    atts = (att, att_sib, att_far, att_diag)

    args = (atts, weights, tokens, grad_out, norms, up_weight, down_weight)
    second, hidden, grad_pre, out_theirs, gs_theirs, _ = middle_part(table, THEIRS, *args, ())
    gs_got = swap(gs_theirs, 1)
    second, hidden, grad_pre, out_mine, gs_mine, middle = middle_part(table, MINE, *args, (second, hidden, grad_pre))
    grad_mid, keep, send, sums_two = norm_two(table, gs_mine, gs_got, middle, grad_out, norms, weights)
    send, second, hidden, grad_pre = lax.optimization_barrier((send, second, hidden, grad_pre))
    got = swap(send, 2)
    width = out_weight.shape[0]
    out_half = add(out_mine, swap(out_theirs, 1)).astype(BF16)

    grad_down = jnp.einsum("tf,td->fd", hidden, grad_out, preferred_element_type=F32).astype(BF16)
    grad_up = jnp.einsum("td,tf->df", second, grad_pre, preferred_element_type=F32).astype(BF16)
    rows = tokens.shape[0] // 2
    pieces = [
        jnp.dot(lax.dynamic_slice_in_dim(a, core * rows, rows, 1), grad_mid, preferred_element_type=F32) for a in atts
    ]
    pieces = [p.astype(BF16) for p in pieces]
    own = add(pieces[0], swap(pieces[1], 1))
    far = add(pieces[2], swap(pieces[3], 1)).astype(BF16)

    got, out_half, far = lax.optimization_barrier((got, out_half, far))
    keep, grad_down, grad_up = lax.optimization_barrier((keep, grad_down, grad_up))
    out_far = swap(out_half, 2)
    grad_down, grad_up = (g.astype(F32) for g in lax.psum((grad_down, grad_up), "dp"))
    grad_att_own = add(keep[:width], got[:width]).astype(BF16)
    grad_att_sib = add(keep[width:], got[width:]).astype(BF16)
    grad_att_other = swap(grad_att_sib, 1)
    grad_out_weight = (own + swap(far, 2).astype(F32)).astype(BF16)

    dq, dk, dv = attend_back(table, info, q, k, v, att, lse, grad_att_own, grad_att_other)
    gf_got = swap(first_grad(table, THEIRS, dq, dk, dv, qkv), 1)
    partial_tokens, sums = norm_one(table, dq, dk, dv, qkv, gf_got, tokens, grad_mid, norms, sums_two)
    partial_tokens, out_far = lax.optimization_barrier((partial_tokens, out_far))
    tokens_far = swap(partial_tokens, 2)
    output = both_halves(core, add(out_half, out_far).astype(BF16))
    sums = sums + swap(sums, 1)
    turn = lambda g: jnp.einsum("te,td->ed", g, first, preferred_element_type=F32).astype(BF16)
    grad_qk, grad_vo, sums, tokens_far = dp_sum_pair(
        table, jnp.concatenate([turn(dq), turn(dk)], 0), jnp.concatenate([turn(dv), grad_out_weight], 0), sums, tokens_far
    )
    sums, tokens_far = lax.optimization_barrier((sums, tokens_far))
    sums = sums + swap(sums, 2)
    grad_tokens = both_halves(core, add(partial_tokens, tokens_far).astype(BF16))
    grad_qkv = jnp.concatenate([grad_qk, grad_vo[:width]], 0).reshape(3, width, -1).swapaxes(1, 2)
    grad_out_weight = grad_vo[width:]
    return (
        output,
        grad_tokens,
        sums[2],
        sums[3],
        grad_qkv,
        grad_out_weight,
        sums[0],
        sums[1],
        grad_up,
        grad_down,
    )


def solution(mesh):
    in_specs = (
        P("dp", None),
        P("dp", None),
        P("dp"),
        P(),
        P(),
        P(None, None, "tensor"),
        P("tensor", None),
        P(),
        P(),
        P(None, "tensor"),
        P("tensor", None),
        P("dp", None),
    )
    out_specs = (
        P("dp", None),
        P("dp", None),
        P(),
        P(),
        P(None, None, "tensor"),
        P("tensor", None),
        P(),
        P(),
        P(None, "tensor"),
        P("tensor", None),
    )
    return jax.shard_map(local, mesh=mesh, in_specs=in_specs, out_specs=out_specs, check_vma=False)
```

time: 373 us -> 346 us (0.928); the launches traced: 379 us -> 346 us
  blocking collectives: 78.5 us -> 0 us
  starting transfers between devices: 11.8 us -> 38.5 us
  waiting for transfers between devices: 112 us -> 121 us
  other arithmetic: 15.9 us -> 21.2 us
  Pallas kernels: 108 us -> 112 us
  local copies, waits for them, and re-layouts: 17.8 us -> 21.8 us
    psum x1 -> x0, blocking collectives: 78.5 us -> none  [local(): lax.psum(jnp.concatenate([sums_one[0:2], sums_two[0:2]], 0), ('dp', 'tens...]
    ppermute x0 -> x15, waiting for transfers between devices: none -> 36.6 us  [dp_swap(): lax.ppermute(value, 'dp', [(d, d ^ distance) for d in range(lax.axis_size...]
    psum x1, waiting for transfers between devices: 28.1 us -> 0.01 us  [local(): lax.psum((grad_down, grad_up), 'dp')]
    ppermute x0 -> x15, starting transfers between devices: none -> 26.3 us  [dp_swap(): lax.ppermute(value, 'dp', [(d, d ^ distance) for d in range(lax.axis_size...]
    pallas_call x0 -> x6, Pallas kernels: none -> 12.3 us  [the longest x3 5.89 us: fold(): pl.pallas_call(partial(fold_kernel, picks, cuts), in_specs=[pl.BlockSpec(...]
    pallas_call x1, Pallas kernels: 22 us -> 14.8 us  [attend(): pl.pallas_call(attend_kernel, grid=(count,), in_specs=[pl.BlockSpec(memor...]
    pallas_call x2 -> x1, Pallas kernels: 10.2 us -> 5.74 us  [first_grad(): pl.pallas_call(first_grad_kernel, grid_spec=pltpu.PrefetchScalarGridSpec(...]
    another operation x2 -> x6, local copies, waits for them, and re-layouts: 0.41 us -> 4.83 us  [the longest x4 2.76 us: local(): norms = jnp.stack([gain_one, shift_one, gain_two, shift_two])]
  transfers between devices with their start and end apart: 19 -> 36, of which waited for: 7 -> 15; matrix products, arithmetic and copies ran while one was open for 11% -> 14% of each run, Pallas kernels for 16% -> 20%
where the time goes in v2:
time: 346 us
  waiting for transfers between devices  121 us (35%)
  Pallas kernels  112 us (32%)
  starting transfers between devices  38.5 us (11%)
  local copies, waits for them, and re-layouts  21.8 us (6%)
  other arithmetic  21.2 us (6%)
  matrix products  17.8 us (5%)
  between operations  15.1 us (4%)
    ppermute x20, waiting for transfers between devices, swap(): return lax.ppermute(value, 'tensor', [(t, t ^ distance) for t in range(4)])  83.9 us
    ppermute x15, waiting for transfers between devices, dp_swap(): lax.ppermute(value, 'dp', [(d, d ^ distance) for d in range(lax.axis_size...  36.6 us
    pallas_call x2, Pallas kernels, middle_part(): pl.pallas_call(middle_kernel, grid_spec=pltpu.PrefetchScalarGridSpec(num_...  29.9 us
    ppermute x15, starting transfers between devices, dp_swap(): lax.ppermute(value, 'dp', [(d, d ^ distance) for d in range(lax.axis_size...  26.3 us
    pallas_call x1, Pallas kernels, attend_back(): pl.pallas_call(attend_back_kernel, grid=(count,), in_specs=[pl.BlockSpec(...  21.8 us
    pallas_call x1, Pallas kernels, attend(): pl.pallas_call(attend_kernel, grid=(count,), in_specs=[pl.BlockSpec(memor...  14.8 us
    ppermute x20, starting transfers between devices, swap(): return lax.ppermute(value, 'tensor', [(t, t ^ distance) for t in range(4)])  12.1 us
    pallas_call x1, Pallas kernels, front(): pl.pallas_call(front_kernel, grid=(count,), in_specs=[pl.BlockSpec(memory...  10.2 us
  transfers between devices with their start and end apart: 36, of which 15 were waited for; matrix products, arithmetic and copies ran while one was open for 14% of the time, Pallas kernels for 20%

profile of v2, /device:TPU:0, one launch (start us, length us, event | category | flops | bytes accessed | tf_op | source)
XLA Modules:
  0.0 346.4 jit_solution(9353339191752844355)
XLA Ops:
  10.3 7.2 %collective-permute-done.1.w2 = bf16[192,768]{1,0:T(8,128)(2,1)S(1)} collective-permute-done((bf16[192,768]{1,0:T(8,128)(2,1)}, bf16[192,768]{1,0:T(8,128)(2,1)S(1)}, u32[]{:S(2)}, u32[]{:S(2)}) %collective-permute-start.1) | collective-permute-done | bytes 294944 | tf_op jit(solution)/shard_map/ppermute | solution.py:672
  21.5 10.2 %front.1 = (bf16[2048,768]{1,0:T(8,128)(2,1)}, bf16[3,2048,128]{2,1,0:T(8,128)(2,1)}, bf16[3,2048,128]{2,1,0:T(8,128)(2,1)}, bf16[3,2048,128]{2,1,0:T(8,128)(2,1)}, s32[8]{0:T(128)}) custom-call(s32[1]{0:T(128)S(6)} %copy.35.live_ref, s32[1,2048]{1,0:T(1,128)} %ids_ref.1, bf16[2048,768]{1,0:T(8,128)(2,1)} %x_ref.7, f32[4,768]{1,0:T(4,128)} %pad_maximum_fusion.3.norm_ref, ...), custom_call_target="tpu_custom_call" | custom-call | flops 10 | bytes 10 | tf_op jit(solution)/shard_map/front/pallas_call | solution.py:94
  31.7 14.8 %attend.1 = (bf16[192,2048]{1,0:T(8,128)(2,1)}, f32[8,8,256]{2,1,0:T(8,128)}) custom-call(s32[8]{0:T(128)} %get-tuple-element.83.info_ref, bf16[3,2048,128]{2,1,0:T(8,128)(2,1)} %get-tuple-element.84.q_ref, bf16[3,2048,128]{2,1,0:T(8,128)(2,1)} %get-tuple-element.85.k_ref, bf16[3,2048,128]{2,1,0:T(8,128)(2,1)} %get-tuple-element.86.v_ref), custom_call_target="tpu_custom_call" | custom-call | flops 20 | bytes 20 | tf_op jit(solution)/shard_map/attend/pallas_call | solution.py:229
  48.6 18.2 %collective-permute-done.4.a2 = bf16[192,2048]{1,0:T(8,128)(2,1)S(1)} collective-permute-done((bf16[192,2048]{1,0:T(8,128)(2,1)}, bf16[192,2048]{1,0:T(8,128)(2,1)S(1)}, u32[]{:S(2)}, u32[]{:S(2)}) %collective-permute-start.4) | collective-permute-done | bytes 786464 | tf_op jit(solution)/shard_map/ppermute | solution.py:672
  70.0 15.0 %middle.2 = (bf16[2048,768]{1,0:T(8,128)(2,1)}, bf16[2048,768]{1,0:T(8,128)(2,1)}, bf16[2048,768]{1,0:T(8,128)(2,1)}, bf16[1024,768]{1,0:T(8,128)(2,1)}, bf16[1024,768]{1,0:T(8,128)(2,1)}, /*index=5*/f32[1024,768]{1,0:T(8,128)}) custom-call(s32[8]{0:T(128)} %and_select_fusion.half_ref.place_ref.table_ref, bf16[192,2048]{1,0:T(8,128)(2,1)} %get-tuple-element.88.a0.att_ref, ...), custom_call_target="tpu_custom_call" | custom-call | flops 14 | bytes 14 | tf_op jit(solution)/shard_map/middle/pallas_call | solution.py:411
  85.5 15.0 %middle.3 = (bf16[2048,768]{1,0:T(8,128)(2,1)}, bf16[2048,768]{1,0:T(8,128)(2,1)}, bf16[2048,768]{1,0:T(8,128)(2,1)}, bf16[1024,768]{1,0:T(8,128)(2,1)}, bf16[1024,768]{1,0:T(8,128)(2,1)}, /*index=5*/f32[1024,768]{1,0:T(8,128)}) custom-call(s32[8]{0:T(128)} %and_select_fusion.half_ref.place_ref.table_re, ...), custom_call_target="tpu_custom_call", output_to_operand_aliasing={{0}: (14, {}), {1}: (15, {}), {2}: (16, {})} | custom-call | flops 14 | bytes 14 | tf_op jit(solution)/shard_map/middle/pallas_call | solution.py:411
  101.7 8.9 %norm_two.1 = (bf16[1024,768]{1,0:T(8,128)(2,1)}, bf16[384,1024]{1,0:T(8,128)(2,1)}, bf16[384,1024]{1,0:T(8,128)(2,1)}, f32[8,768]{1,0:T(8,128)}) custom-call(s32[8]{0:T(128)} %and_select_fusion.half_ref.place_ref.table_ref, bf16[1024,768]{1,0:T(8,128)(2,1)} %get-tuple-element.95.own_ref, bf16[1024,768]{1,0:T(8,128)(2,1)} %copy-done.19, ...), custom_call_target="tpu_custom_call" | custom-call | flops 8 | bytes 8 | tf_op jit(solution)/shard_map/norm_two/pallas_call | solution.py:454
  110.6 5.8 %convolution_convert_fusion.1 = bf16[768,768]{1,0:T(8,128)(2,1)} fusion(bf16[2048,768]{1,0:T(8,128)(2,1)} %get-tuple-element.109, bf16[2048,768]{1,0:T(8,128)(2,1)S(1)} %copy-done.1), kind=kOutput, calls=%fused_computation.5 | convolution fusion | flops 2416508928 | bytes 7471104 | tf_op jit(solution)/shard_map/tf,td->fd/dot_general | solution.py:728
  116.4 3.9 %convolution_convert_fusion = bf16[768,768]{1,0:T(8,128)(2,1)} fusion(bf16[2048,768]{1,0:T(8,128)(2,1)S(1)} %copy-done.12, bf16[2048,768]{1,0:T(8,128)(2,1)S(1)} %copy-done.13), kind=kOutput, calls=%fused_computation.4 | convolution fusion | flops 2416508928 | bytes 7471104 | tf_op jit(solution)/shard_map/td,tf->df/dot_general | solution.py:729
  126.2 13.7 %collective-permute-done.7 = bf16[384,1024]{1,0:T(8,128)(2,1)S(1)} collective-permute-done((bf16[384,1024]{1,0:T(8,128)(2,1)S(1)}, bf16[384,1024]{1,0:T(8,128)(2,1)S(1)}, u32[]{:S(2)}, u32[]{:S(2)}) %collective-permute-start.7) | collective-permute-done | bytes 786464 | tf_op jit(solution)/shard_map/ppermute | solution.py:672
  143.4 21.8 %attend_back.1 = (bf16[2048,192]{1,0:T(8,128)(2,1)}, bf16[2048,192]{1,0:T(8,128)(2,1)}, bf16[2048,192]{1,0:T(8,128)(2,1)}) custom-call(s32[8]{0:T(128)} %and_select_fusion.half_ref.place_ref.table_ref, s32[8]{0:T(128)} %get-tuple-element.83.info_ref, bf16[3,2048,128]{2,1,0:T(8,128)(2,1)} %get-tuple-element.84.q_ref, ...), custom_call_target="tpu_custom_call" | custom-call | flops 28 | bytes 28 | tf_op jit(solution)/shard_map/attend_back/pallas_call | solution.py:344
  165.2 5.7 %first_grad.1 = bf16[1024,768]{1,0:T(8,128)(2,1)} custom-call(s32[8]{0:T(128)} %and_select_fusion.half_ref.place_ref.table_ref, bf16[2048,192]{1,0:T(8,128)(2,1)} %get-tuple-element.114.dq_ref, bf16[2048,192]{1,0:T(8,128)(2,1)} %get-tuple-element.115.dk_ref, bf16[2048,192]{1,0:T(8,128)(2,1)} %get-tuple-element.116.dv_ref, bf16[3,192,768]{2,1,0:T(8,128)(2,1)} %bitcast.19), custom_call_target="tpu_custom_call" | custom-call | flops 4 | bytes 4 | tf_op jit(solution)/shard_map/first_grad/pallas_call | solution.py:490
  175.0 39.3 %collective-permute-done.18 = bf16[192,768]{1,0:T(8,128)(2,1)S(1)} collective-permute-done((bf16[192,768]{1,0:T(8,128)(2,1)S(1)}, bf16[192,768]{1,0:T(8,128)(2,1)S(1)}, u32[]{:S(2)}, u32[]{:S(2)}) %collective-permute-start.18) | collective-permute-done | bytes 294944 | tf_op jit(solution)/shard_map/ppermute | solution.py:672
  217.5 7.7 %norm_one.1 = (bf16[1024,768]{1,0:T(8,128)(2,1)}, f32[8,768]{1,0:T(8,128)}) custom-call(s32[8]{0:T(128)} %and_select_fusion.half_ref.place_ref.table_ref, bf16[2048,192]{1,0:T(8,128)(2,1)} %get-tuple-element.114.dq_ref, bf16[2048,192]{1,0:T(8,128)(2,1)} %get-tuple-element.115.dk_ref, bf16[2048,192]{1,0:T(8,128)(2,1)} %get-tuple-element.116.dv_ref, ...), custom_call_target="tpu_custom_call" | custom-call | flops 10 | bytes 10 | tf_op jit(solution)/shard_map/norm_one/pallas_call | solution.py:523
  231.0 5.2 %collective-permute-start.19 = (bf16[192,768]{1,0:T(8,128)(2,1)S(1)}, bf16[192,768]{1,0:T(8,128)(2,1)S(1)}, u32[]{:S(2)}, u32[]{:S(2)}) collective-permute-start(bf16[192,768]{1,0:T(8,128)(2,1)S(1)} %fusion.11), channel_id=1, source_target_pairs={{0,8},{4,12},{8,0},{12,4},{16,24},{20,28},{24,16},{28,20},{1,9},{5... | collective-permute-start | bytes 884744 | tf_op jit(solution)/shard_map/ppermute | solution.py:632
  236.4 7.6 %collective-permute-start.16 = (bf16[192,768]{1,0:T(8,128)(2,1)S(1)}, bf16[192,768]{1,0:T(8,128)(2,1)S(1)}, u32[]{:S(2)}, u32[]{:S(2)}) collective-permute-start(bf16[192,768]{1,0:T(8,128)(2,1)S(1)} %fusion.12), channel_id=1, source_target_pairs={{0,4},{4,0},{8,12},{12,8},{16,20},{20,16},{24,28},{28,24},{1,5},{5... | collective-permute-start | bytes 884744 | tf_op jit(solution)/shard_map/ppermute | solution.py:632
  246.8 3.9 %constant_dynamic-update-slice_fusion.3 = (bf16[2048,768]{1,0:T(8,128)(2,1)}, bf16[1024,768]{1,0:T(8,128)(2,1)}) fusion(bf16[2048,768]{1,0:T(8,128)(2,1)} %broadcast.18.clone, s32[]{:T(128)S(6)} %select_n.54, bf16[1024,768]{1,0:T(8,128)(2,1)} %collective-permute-done.12, bf16[1024,768]{1,0:T(8,128)(2,1)} %add_convert_fusion.2), kind=kLoop, calls=%fused_computation.44 | loop fusion | flops 3145728 | bytes 6291460 | tf_op jit(solution)/shard_map/dynamic_update_slice | solution.py:683
  261.1 10.5 %collective-permute-done.20 = f32[8,768]{1,0:T(8,128)S(1)} collective-permute-done((f32[8,768]{1,0:T(8,128)S(1)}, f32[8,768]{1,0:T(8,128)S(1)}, u32[]{:S(2)}, u32[]{:S(2)}) %collective-permute-start.20) | collective-permute-done | bytes 24608 | tf_op jit(solution)/shard_map/ppermute | solution.py:632
  271.7 3.6 %collective-permute-done.22.refs_2_ = bf16[96,768]{1,0:T(8,128)(2,1)S(1)} collective-permute-done((bf16[96,768]{1,0:T(8,128)(2,1)}, bf16[96,768]{1,0:T(8,128)(2,1)S(1)}, u32[]{:S(2)}, u32[]{:S(2)}) %collective-permute-start.22) | collective-permute-done | bytes 147488 | tf_op jit(solution)/shard_map/ppermute | solution.py:632
  277.8 3.2 collective-permute-start.25
  283.9 7.4 %collective-permute-done.23 = f32[8,768]{1,0:T(8,128)S(1)} collective-permute-done((f32[8,768]{1,0:T(8,128)S(1)}, f32[8,768]{1,0:T(8,128)S(1)}, u32[]{:S(2)}, u32[]{:S(2)}) %collective-permute-start.23) | collective-permute-done | bytes 24608 | tf_op jit(solution)/shard_map/ppermute | solution.py:632
  293.9 3.5 %constant_dynamic-update-slice_fusion.1 = (bf16[2048,768]{1,0:T(8,128)(2,1)S(1)}, bf16[1024,768]{1,0:T(8,128)(2,1)}) fusion(bf16[2048,768]{1,0:T(8,128)(2,1)S(1)} %broadcast.18.clone.1, s32[]{:T(128)S(6)} %select_n.54, bf16[1024,768]{1,0:T(8,128)(2,1)} %collective-permute-done.26, bf16[1024,768]{1,0:T(8,128)(2,1)} %get-tuple-element.120), kind=kLoop, calls=%fused_computation.40 | loop fusion | flops 3145728 | bytes 6291460 | tf_op jit(solution)/shard_map/dynamic_update_slice | solution.py:683
  299.5 3.5 %collective-permute-done.29.refs_1_ = bf16[48,768]{1,0:T(8,128)(2,1)S(1)} collective-permute-done((bf16[48,768]{1,0:T(8,128)(2,1)S(1)}, bf16[48,768]{1,0:T(8,128)(2,1)S(1)}, u32[]{:S(2)}, u32[]{:S(2)}) %collective-permute-start.29) | collective-permute-done | bytes 73760 | tf_op jit(solution)/shard_map/ppermute | solution.py:632
  307.4 7.3 %collective-permute-done.31.refs_1_ = bf16[96,768]{1,0:T(8,128)(2,1)S(1)} collective-permute-done((bf16[96,768]{1,0:T(8,128)(2,1)}, bf16[96,768]{1,0:T(8,128)(2,1)S(1)}, u32[]{:S(2)}, u32[]{:S(2)}) %collective-permute-start.31) | collective-permute-done | bytes 147488 | tf_op jit(solution)/shard_map/ppermute | solution.py:632
  (182 shorter events, 88.3 us)
Async XLA Ops:
  7.2 313.2 %all-reduce.3.cloned.1.call-start = ((), (), s32[]{:S(2)}) async-start(), calls=%async_computation | async-start | bytes 4718592 | tf_op jit(solution)/shard_map/psum | solution.py:741
  7.2 10.3 %collective-permute-start.1 = (bf16[192,768]{1,0:T(8,128)(2,1)}, bf16[192,768]{1,0:T(8,128)(2,1)S(1)}, u32[]{:S(2)}, u32[]{:S(2)}) collective-permute-start(bf16[192,768]{1,0:T(8,128)(2,1)} %w0.5), channel_id=1, source_target_pairs={{0,2},{1,3},{2,0},{3,1},{4,6},{5,7},{6,4},{7,5},{8,10},{9,11},{10,... | collective-permute-start | bytes 884744 | tf_op jit(solution)/shard_map/ppermute | solution.py:672
  10.3 36.3 %collective-permute-start = (bf16[192,768]{1,0:T(8,128)(2,1)}, bf16[192,768]{1,0:T(8,128)(2,1)S(1)}, u32[]{:S(2)}, u32[]{:S(2)}) collective-permute-start(bf16[192,768]{1,0:T(8,128)(2,1)} %w0.5), channel_id=1, source_target_pairs={{0,1},{1,0},{2,3},{3,2},{4,5},{5,4},{6,7},{7,6},{8,9},{9,8},{10,11... | collective-permute-start | bytes 884744 | tf_op jit(solution)/shard_map/ppermute | solution.py:672
  17.5 29.1 %collective-permute-start.2 = (bf16[192,768]{1,0:T(8,128)(2,1)S(1)}, bf16[192,768]{1,0:T(8,128)(2,1)S(1)}, u32[]{:S(2)}, u32[]{:S(2)}) collective-permute-start(bf16[192,768]{1,0:T(8,128)(2,1)S(1)} %collective-permute-done.1.w2), channel_id=1, source_target_pairs={{0,1},{1,0},{2,3},{3,2},{4,5},{5,4},{6,7},{7,6},{8,9},{9,8},{10,11... | collective-permute-start | bytes 884744 | tf_op jit(solution)/shard_map/ppermute | solution.py:672
  46.6 20.2 %collective-permute-start.4 = (bf16[192,2048]{1,0:T(8,128)(2,1)}, bf16[192,2048]{1,0:T(8,128)(2,1)S(1)}, u32[]{:S(2)}, u32[]{:S(2)}) collective-permute-start(bf16[192,2048]{1,0:T(8,128)(2,1)} %get-tuple-element.88.a0.att_ref), channel_id=1, source_target_pairs={{0,2},{1,3},{2,0},{3,1},{4,6},{5,7},{6,4},{7,5},{8,10},{9,11},{10,... | collective-permute-start | bytes 2359304 | tf_op jit(solution)/shard_map/ppermute | solution.py:672
  48.4 19.3 %collective-permute-start.3 = (bf16[192,2048]{1,0:T(8,128)(2,1)}, bf16[192,2048]{1,0:T(8,128)(2,1)S(1)}, u32[]{:S(2)}, u32[]{:S(2)}) collective-permute-start(bf16[192,2048]{1,0:T(8,128)(2,1)} %get-tuple-element.88.a0.att_ref), channel_id=1, source_target_pairs={{0,1},{1,0},{2,3},{3,2},{4,5},{5,4},{6,7},{7,6},{8,9},{9,8},{10,11... | collective-permute-start | bytes 2359304 | tf_op jit(solution)/shard_map/ppermute | solution.py:672
  85.0 15.6 %collective-permute-start.6 = (bf16[1024,768]{1,0:T(8,128)(2,1)}, bf16[1024,768]{1,0:T(8,128)(2,1)S(1)}, u32[]{:S(2)}, u32[]{:S(2)}) collective-permute-start(bf16[1024,768]{1,0:T(8,128)(2,1)} %get-tuple-element.96), channel_id=1, source_target_pairs={{0,1},{1,0},{2,3},{3,2},{4,5},{5,4},{6,7},{7,6},{8,9},{9,8},{10,11... | collective-permute-start | bytes 4718600 | tf_op jit(solution)/shard_map/ppermute | solution.py:672
  85.2 37.4 %collective-permute-start.8 = (bf16[1024,768]{1,0:T(8,128)(2,1)}, bf16[1024,768]{1,0:T(8,128)(2,1)}, u32[]{:S(2)}, u32[]{:S(2)}) collective-permute-start(bf16[1024,768]{1,0:T(8,128)(2,1)} %get-tuple-element.104), channel_id=1, source_target_pairs={{0,1},{1,0},{2,3},{3,2},{4,5},{5,4},{6,7},{7,6},{8,9},{9,8},{10,11... | collective-permute-start | bytes 4718600 | tf_op jit(solution)/shard_map/ppermute | solution.py:672
  120.2 19.6 %collective-permute-start.7 = (bf16[384,1024]{1,0:T(8,128)(2,1)S(1)}, bf16[384,1024]{1,0:T(8,128)(2,1)S(1)}, u32[]{:S(2)}, u32[]{:S(2)}) collective-permute-start(bf16[384,1024]{1,0:T(8,128)(2,1)S(1)} %copy-done.40), channel_id=1, source_target_pairs={{0,2},{1,3},{2,0},{3,1},{4,6},{5,7},{6,4},{7,5},{8,10},{9,11},{10,... | collective-permute-start | bytes 2359304 | tf_op jit(solution)/shard_map/ppermute | solution.py:672
  171.0 46.6 %collective-permute-start.11 = (bf16[1024,768]{1,0:T(8,128)(2,1)}, bf16[1024,768]{1,0:T(8,128)(2,1)}, u32[]{:S(2)}, u32[]{:S(2)}) collective-permute-start(bf16[1024,768]{1,0:T(8,128)(2,1)} %first_grad.1), channel_id=1, source_target_pairs={{0,1},{1,0},{2,3},{3,2},{4,5},{5,4},{6,7},{7,6},{8,9},{9,8},{10,11... | collective-permute-start | bytes 4718600 | tf_op jit(solution)/shard_map/ppermute | solution.py:672
  171.1 54.2 %collective-permute-start.12 = (bf16[1024,768]{1,0:T(8,128)(2,1)}, bf16[1024,768]{1,0:T(8,128)(2,1)}, u32[]{:S(2)}, u32[]{:S(2)}) collective-permute-start(bf16[1024,768]{1,0:T(8,128)(2,1)} %add_convert_fusion.2), channel_id=1, source_target_pairs={{0,2},{1,3},{2,0},{3,1},{4,6},{5,7},{6,4},{7,5},{8,10},{9,11},{10,... | collective-permute-start | bytes 4718600 | tf_op jit(solution)/shard_map/ppermute | solution.py:672
  173.5 40.8 %collective-permute-start.18 = (bf16[192,768]{1,0:T(8,128)(2,1)S(1)}, bf16[192,768]{1,0:T(8,128)(2,1)S(1)}, u32[]{:S(2)}, u32[]{:S(2)}) collective-permute-start(bf16[192,768]{1,0:T(8,128)(2,1)S(1)} %fusion.2), channel_id=1, source_target_pairs={{0,2},{1,3},{2,0},{3,1},{4,6},{5,7},{6,4},{7,5},{8,10},{9,11},{10,... | collective-permute-start | bytes 884744 | tf_op jit(solution)/shard_map/ppermute | solution.py:672
  225.3 68.4 %collective-permute-start.26 = (bf16[1024,768]{1,0:T(8,128)(2,1)}, bf16[1024,768]{1,0:T(8,128)(2,1)}, u32[]{:S(2)}, u32[]{:S(2)}) collective-permute-start(bf16[1024,768]{1,0:T(8,128)(2,1)} %get-tuple-element.120), channel_id=1, source_target_pairs={{0,2},{1,3},{2,0},{3,1},{4,6},{5,7},{6,4},{7,5},{8,10},{9,11},{10,... | collective-permute-start | bytes 4718600 | tf_op jit(solution)/shard_map/ppermute | solution.py:672
  231.0 24.3 %collective-permute-start.19 = (bf16[192,768]{1,0:T(8,128)(2,1)S(1)}, bf16[192,768]{1,0:T(8,128)(2,1)S(1)}, u32[]{:S(2)}, u32[]{:S(2)}) collective-permute-start(bf16[192,768]{1,0:T(8,128)(2,1)S(1)} %fusion.11), channel_id=1, source_target_pairs={{0,8},{4,12},{8,0},{12,4},{16,24},{20,28},{24,16},{28,20},{1,9},{5... | collective-permute-start | bytes 884744 | tf_op jit(solution)/shard_map/ppermute | solution.py:632
  236.4 18.9 %collective-permute-start.16 = (bf16[192,768]{1,0:T(8,128)(2,1)S(1)}, bf16[192,768]{1,0:T(8,128)(2,1)S(1)}, u32[]{:S(2)}, u32[]{:S(2)}) collective-permute-start(bf16[192,768]{1,0:T(8,128)(2,1)S(1)} %fusion.12), channel_id=1, source_target_pairs={{0,4},{4,0},{8,12},{12,8},{16,20},{20,16},{24,28},{28,24},{1,5},{5... | collective-permute-start | bytes 884744 | tf_op jit(solution)/shard_map/ppermute | solution.py:632
  250.7 74.2 %collective-permute-start.13 = (bf16[1024,768]{1,0:T(8,128)(2,1)}, bf16[1024,768]{1,0:T(8,128)(2,1)}, u32[]{:S(2)}, u32[]{:S(2)}) collective-permute-start(bf16[1024,768]{1,0:T(8,128)(2,1)} %get-tuple-element.165), channel_id=1, source_target_pairs={{0,1},{1,0},{2,3},{3,2},{4,5},{5,4},{6,7},{7,6},{8,9},{9,8},{10,11... | collective-permute-start | bytes 4718600 | tf_op jit(solution)/shard_map/ppermute | solution.py:672
  259.1 12.6 %collective-permute-start.21 = (bf16[96,768]{1,0:T(8,128)(2,1)}, bf16[96,768]{1,0:T(8,128)(2,1)S(1)}, u32[]{:S(2)}, u32[]{:S(2)}) collective-permute-start(bf16[96,768]{1,0:T(8,128)(2,1)} %get-tuple-element.127), channel_id=1, source_target_pairs={{0,8},{4,12},{8,0},{12,4},{16,24},{20,28},{24,16},{28,20},{1,9},{5... | collective-permute-start | bytes 442376 | tf_op jit(solution)/shard_map/ppermute | solution.py:632
  260.9 14.4 %collective-permute-start.22 = (bf16[96,768]{1,0:T(8,128)(2,1)}, bf16[96,768]{1,0:T(8,128)(2,1)S(1)}, u32[]{:S(2)}, u32[]{:S(2)}) collective-permute-start(bf16[96,768]{1,0:T(8,128)(2,1)} %get-tuple-element.128), channel_id=1, source_target_pairs={{0,16},{4,20},{8,24},{12,28},{16,0},{20,4},{24,8},{28,12},{1,17},{... | collective-permute-start | bytes 442376 | tf_op jit(solution)/shard_map/ppermute | solution.py:632
  260.9 10.8 %collective-permute-start.20 = (f32[8,768]{1,0:T(8,128)S(1)}, f32[8,768]{1,0:T(8,128)S(1)}, u32[]{:S(2)}, u32[]{:S(2)}) collective-permute-start(f32[8,768]{1,0:T(8,128)S(1)} %add.101), channel_id=1, source_target_pairs={{0,8},{4,12},{8,0},{12,4},{16,24},{20,28},{24,16},{28,20},{1,9},{5... | collective-permute-start | bytes 73736 | tf_op jit(solution)/shard_map/ppermute | solution.py:632
  277.8 13.5 %collective-permute-start.24 = (bf16[48,768]{1,0:T(8,128)(2,1)}, bf16[48,768]{1,0:T(8,128)(2,1)S(1)}, u32[]{:S(2)}, u32[]{:S(2)}) collective-permute-start(bf16[48,768]{1,0:T(8,128)(2,1)} %get-tuple-element.134), channel_id=1, source_target_pairs={{0,16},{4,20},{8,24},{12,28},{16,0},{20,4},{24,8},{28,12},{1,17},{... | collective-permute-start | bytes 221192 | tf_op jit(solution)/shard_map/ppermute | solution.py:632
  277.8 13.5 %collective-permute-start.25 = (bf16[48,768]{1,0:T(8,128)(2,1)}, bf16[48,768]{1,0:T(8,128)(2,1)S(1)}, u32[]{:S(2)}, u32[]{:S(2)}) collective-permute-start(bf16[48,768]{1,0:T(8,128)(2,1)} %get-tuple-element.135), channel_id=1, source_target_pairs={{0,4},{4,0},{8,12},{12,8},{16,20},{20,16},{24,28},{28,24},{1,5},{5... | collective-permute-start | bytes 221192 | tf_op jit(solution)/shard_map/ppermute | solution.py:632
  281.0 10.3 %collective-permute-start.23 = (f32[8,768]{1,0:T(8,128)S(1)}, f32[8,768]{1,0:T(8,128)S(1)}, u32[]{:S(2)}, u32[]{:S(2)}) collective-permute-start(f32[8,768]{1,0:T(8,128)S(1)} %add.108), channel_id=1, source_target_pairs={{0,16},{4,20},{8,24},{12,28},{16,0},{20,4},{24,8},{28,12},{1,17},{... | collective-permute-start | bytes 73736 | tf_op jit(solution)/shard_map/ppermute | solution.py:632
  297.4 38.9 %collective-permute-start.27 = (bf16[1024,768]{1,0:T(8,128)(2,1)}, bf16[1024,768]{1,0:T(8,128)(2,1)}, u32[]{:S(2)}, u32[]{:S(2)}) collective-permute-start(bf16[1024,768]{1,0:T(8,128)(2,1)} %get-tuple-element.163), channel_id=1, source_target_pairs={{0,1},{1,0},{2,3},{3,2},{4,5},{5,4},{6,7},{7,6},{8,9},{9,8},{10,11... | collective-permute-start | bytes 4718600 | tf_op jit(solution)/shard_map/ppermute | solution.py:672
  318.4 11.0 %collective-permute-start.33 = (bf16[192,768]{1,0:T(8,128)(2,1)}, bf16[192,768]{1,0:T(8,128)(2,1)S(1)}, u32[]{:S(2)}, u32[]{:S(2)}) collective-permute-start(bf16[192,768]{1,0:T(8,128)(2,1)} %get-tuple-element.150.refs_0_), channel_id=1, source_target_pairs={{0,4},{4,0},{8,12},{12,8},{16,20},{20,16},{24,28},{28,24},{1,5},{5... | collective-permute-start | bytes 884744 | tf_op jit(solution)/shard_map/ppermute | solution.py:632
  (53 other events, 365.0 us)
Sparse Core Ops, SparseCore 0:
  173.9 127.4 all-reduce.2

commit v3 on v2

--- a/solution.py
+++ b/solution.py
@@ -369,7 +369,7 @@
             VMEM((heads, BLK, BLK), BF16),
             VMEM((heads, BLK, BLK), BF16),
         ],
-        cost_estimate=cost(28),
+        cost_estimate=cost(10**11),
         name="attend_back",
     )(half, info, q, k, v, att, lse, own, other)
 
@@ -735,19 +735,21 @@
     own = add(pieces[0], swap(pieces[1], 1))
     far = add(pieces[2], swap(pieces[3], 1)).astype(BF16)
 
-    got, out_half, far = lax.optimization_barrier((got, out_half, far))
-    keep, grad_down, grad_up = lax.optimization_barrier((keep, grad_down, grad_up))
+    got, out_half = lax.optimization_barrier((got, out_half))
+    keep, grad_down, grad_up, own, far = lax.optimization_barrier((keep, grad_down, grad_up, own, far))
+    far = swap(far, 2)
     out_far = swap(out_half, 2)
     grad_down, grad_up = (g.astype(F32) for g in lax.psum((grad_down, grad_up), "dp"))
     grad_att_own = add(keep[:width], got[:width]).astype(BF16)
     grad_att_sib = add(keep[width:], got[width:]).astype(BF16)
     grad_att_other = swap(grad_att_sib, 1)
-    grad_out_weight = (own + swap(far, 2).astype(F32)).astype(BF16)
 
     dq, dk, dv = attend_back(table, info, q, k, v, att, lse, grad_att_own, grad_att_other)
+    dq, out_far = lax.optimization_barrier((dq, out_far))
     gf_got = swap(first_grad(table, THEIRS, dq, dk, dv, qkv), 1)
     partial_tokens, sums = norm_one(table, dq, dk, dv, qkv, gf_got, tokens, grad_mid, norms, sums_two)
-    partial_tokens, out_far = lax.optimization_barrier((partial_tokens, out_far))
+    own, far, dq, dk, dv, partial_tokens = lax.optimization_barrier((own, far, dq, dk, dv, partial_tokens))
+    grad_out_weight = (own + far.astype(F32)).astype(BF16)
     tokens_far = swap(partial_tokens, 2)
     output = both_halves(core, add(out_half, out_far).astype(BF16))
     sums = sums + swap(sums, 1)

time: 346 us -> 338 us (0.977)
  waiting for transfers between devices: 121 us -> 101 us
  matrix products: 17.8 us -> 22.7 us
    ppermute x20, waiting for transfers between devices: 83.9 us -> 41 us  [swap(): return lax.ppermute(value, 'tensor', [(t, t ^ distance) for t in range(4)])]
    psum x1, waiting for transfers between devices: 0.01 us -> 20.2 us  [local(): lax.psum((grad_down, grad_up), 'dp')]
    dot_general x4, matrix products: 1.92 us -> 7.77 us  [local(): jnp.dot(lax.dynamic_slice_in_dim(a, core * rows, rows, 1), grad_mid, pref...]
    ppermute x20, starting transfers between devices: 12.1 us -> 15.7 us  [swap(): return lax.ppermute(value, 'tensor', [(t, t ^ distance) for t in range(4)])]
    unnamed x82 -> x86, local copies, waits for them, and re-layouts: 9.89 us -> 11.6 us
  transfers between devices with their start and end apart: 36 -> 36, of which waited for: 15 -> 15; matrix products, arithmetic and copies ran while one was open for 14% -> 15% of each run, Pallas kernels for 20% -> 27%
where the time goes in v3:
time: 338 us; the launch traced here: 337 us
  Pallas kernels  112 us (33%)
  waiting for transfers between devices  101 us (30%)
  starting transfers between devices  41.8 us (12%)
  local copies, waits for them, and re-layouts  23.5 us (7%)
  matrix products  22.7 us (7%)
  other arithmetic  20.1 us (6%)
  between operations  15.1 us (4%)
    ppermute x20, waiting for transfers between devices, swap(): return lax.ppermute(value, 'tensor', [(t, t ^ distance) for t in range(4)])  41 us
    ppermute x15, waiting for transfers between devices, dp_swap(): lax.ppermute(value, 'dp', [(d, d ^ distance) for d in range(lax.axis_size...  39.8 us
    pallas_call x2, Pallas kernels, middle_part(): pl.pallas_call(middle_kernel, grid_spec=pltpu.PrefetchScalarGridSpec(num_...  29.9 us
    ppermute x15, starting transfers between devices, dp_swap(): lax.ppermute(value, 'dp', [(d, d ^ distance) for d in range(lax.axis_size...  26.1 us
    pallas_call x1, Pallas kernels, attend_back(): pl.pallas_call(attend_back_kernel, grid=(count,), in_specs=[pl.BlockSpec(...  22.8 us
    psum x1, waiting for transfers between devices, local(): lax.psum((grad_down, grad_up), 'dp')  20.2 us
    ppermute x20, starting transfers between devices, swap(): return lax.ppermute(value, 'tensor', [(t, t ^ distance) for t in range(4)])  15.7 us
    pallas_call x1, Pallas kernels, attend(): pl.pallas_call(attend_kernel, grid=(count,), in_specs=[pl.BlockSpec(memor...  15.1 us
  transfers between devices with their start and end apart: 36, of which 15 were waited for; matrix products, arithmetic and copies ran while one was open for 15% of the time, Pallas kernels for 27%

profile of v3, /device:TPU:0, one launch (start us, length us, event | category | flops | bytes accessed | tf_op | source)
XLA Modules:
  0.0 336.7 jit_solution(3399557450355151230)
XLA Ops:
  7.2 3.0 collective-permute-start.1
  10.3 7.2 %collective-permute-done.1.w2 = bf16[192,768]{1,0:T(8,128)(2,1)S(1)} collective-permute-done((bf16[192,768]{1,0:T(8,128)(2,1)}, bf16[192,768]{1,0:T(8,128)(2,1)S(1)}, u32[]{:S(2)}, u32[]{:S(2)}) %collective-permute-start.1) | collective-permute-done | bytes 294944 | tf_op jit(solution)/shard_map/ppermute | solution.py:672
  21.5 10.2 %front.1 = (bf16[2048,768]{1,0:T(8,128)(2,1)}, bf16[3,2048,128]{2,1,0:T(8,128)(2,1)}, bf16[3,2048,128]{2,1,0:T(8,128)(2,1)}, bf16[3,2048,128]{2,1,0:T(8,128)(2,1)}, s32[8]{0:T(128)}) custom-call(s32[1]{0:T(128)S(6)} %copy.35.live_ref, s32[1,2048]{1,0:T(1,128)} %ids_ref.1, bf16[2048,768]{1,0:T(8,128)(2,1)} %x_ref.7, f32[4,768]{1,0:T(4,128)} %pad_maximum_fusion.3.norm_ref, ...), custom_call_target="tpu_custom_call" | custom-call | flops 10 | bytes 10 | tf_op jit(solution)/shard_map/front/pallas_call | solution.py:94
  31.7 15.1 %attend.1 = (bf16[192,2048]{1,0:T(8,128)(2,1)}, f32[8,8,256]{2,1,0:T(8,128)}) custom-call(s32[8]{0:T(128)} %get-tuple-element.90.info_ref, bf16[3,2048,128]{2,1,0:T(8,128)(2,1)} %get-tuple-element.91.q_ref, bf16[3,2048,128]{2,1,0:T(8,128)(2,1)} %get-tuple-element.92.k_ref, bf16[3,2048,128]{2,1,0:T(8,128)(2,1)} %get-tuple-element.93.v_ref), custom_call_target="tpu_custom_call" | custom-call | flops 20 | bytes 20 | tf_op jit(solution)/shard_map/attend/pallas_call | solution.py:229
  48.8 18.2 %collective-permute-done.4.a2 = bf16[192,2048]{1,0:T(8,128)(2,1)S(1)} collective-permute-done((bf16[192,2048]{1,0:T(8,128)(2,1)}, bf16[192,2048]{1,0:T(8,128)(2,1)S(1)}, u32[]{:S(2)}, u32[]{:S(2)}) %collective-permute-start.4) | collective-permute-done | bytes 786464 | tf_op jit(solution)/shard_map/ppermute | solution.py:672
  70.3 15.0 %middle.2 = (bf16[2048,768]{1,0:T(8,128)(2,1)}, bf16[2048,768]{1,0:T(8,128)(2,1)}, bf16[2048,768]{1,0:T(8,128)(2,1)}, bf16[1024,768]{1,0:T(8,128)(2,1)}, bf16[1024,768]{1,0:T(8,128)(2,1)}, /*index=5*/f32[1024,768]{1,0:T(8,128)}) custom-call(s32[8]{0:T(128)} %and_select_fusion.half_ref.place_ref.table_ref, bf16[192,2048]{1,0:T(8,128)(2,1)} %get-tuple-element.95.a0.att_ref, ...), custom_call_target="tpu_custom_call" | custom-call | flops 14 | bytes 14 | tf_op jit(solution)/shard_map/middle/pallas_call | solution.py:411
  85.8 15.0 %middle.3 = (bf16[2048,768]{1,0:T(8,128)(2,1)}, bf16[2048,768]{1,0:T(8,128)(2,1)}, bf16[2048,768]{1,0:T(8,128)(2,1)}, bf16[1024,768]{1,0:T(8,128)(2,1)}, bf16[1024,768]{1,0:T(8,128)(2,1)}, /*index=5*/f32[1024,768]{1,0:T(8,128)}) custom-call(s32[8]{0:T(128)} %and_select_fusion.half_ref.place_ref.table_re, ...), custom_call_target="tpu_custom_call", output_to_operand_aliasing={{0}: (14, {}), {1}: (15, {}), {2}: (16, {})} | custom-call | flops 14 | bytes 14 | tf_op jit(solution)/shard_map/middle/pallas_call | solution.py:411
  101.9 8.8 %norm_two.1 = (bf16[1024,768]{1,0:T(8,128)(2,1)}, bf16[384,1024]{1,0:T(8,128)(2,1)}, bf16[384,1024]{1,0:T(8,128)(2,1)}, f32[8,768]{1,0:T(8,128)}) custom-call(s32[8]{0:T(128)} %and_select_fusion.half_ref.place_ref.table_ref, bf16[1024,768]{1,0:T(8,128)(2,1)} %get-tuple-element.102.own_ref, bf16[1024,768]{1,0:T(8,128)(2,1)} %copy-done.21, ...), custom_call_target="tpu_custom_call" | custom-call | flops 8 | bytes 8 | tf_op jit(solution)/shard_map/norm_two/pallas_call | solution.py:454
  116.3 6.6 %convolution_convert_fusion.1 = bf16[768,768]{1,0:T(8,128)(2,1)} fusion(bf16[2048,768]{1,0:T(8,128)(2,1)} %get-tuple-element.115, bf16[2048,768]{1,0:T(8,128)(2,1)} %go_ref.5), kind=kOutput, calls=%fused_computation.5 | convolution fusion | flops 2416508928 | bytes 7471104 | tf_op jit(solution)/shard_map/tf,td->fd/dot_general | solution.py:728
  122.9 3.8 %convolution_convert_fusion = bf16[768,768]{1,0:T(8,128)(2,1)} fusion(bf16[2048,768]{1,0:T(8,128)(2,1)S(1)} %copy-done.11, bf16[2048,768]{1,0:T(8,128)(2,1)S(1)} %copy-done.12), kind=kOutput, calls=%fused_computation.4 | convolution fusion | flops 2416508928 | bytes 7471104 | tf_op jit(solution)/shard_map/td,tf->df/dot_general | solution.py:729
  139.1 22.8 %attend_back.1 = (bf16[2048,192]{1,0:T(8,128)(2,1)}, bf16[2048,192]{1,0:T(8,128)(2,1)}, bf16[2048,192]{1,0:T(8,128)(2,1)}) custom-call(s32[8]{0:T(128)} %and_select_fusion.half_ref.place_ref.table_ref, s32[8]{0:T(128)} %get-tuple-element.90.info_ref, bf16[3,2048,128]{2,1,0:T(8,128)(2,1)} %get-tuple-element.91.q_ref, ...), custom_call_target="tpu_custom_call" | custom-call | flops 99999997952 | bytes 99999997952 | tf_op jit(solution)/shard_map/attend_back/pallas_call | solution.py:344
  161.9 11.5 %collective-permute-done.12 = bf16[1024,768]{1,0:T(8,128)(2,1)S(1)} collective-permute-done((bf16[1024,768]{1,0:T(8,128)(2,1)S(1)}, bf16[1024,768]{1,0:T(8,128)(2,1)S(1)}, u32[]{:S(2)}, u32[]{:S(2)}) %collective-permute-start.12) | collective-permute-done | bytes 1572896 | tf_op jit(solution)/shard_map/ppermute | solution.py:672
  174.5 5.7 %first_grad.1 = bf16[1024,768]{1,0:T(8,128)(2,1)} custom-call(s32[8]{0:T(128)} %and_select_fusion.half_ref.place_ref.table_ref, bf16[2048,192]{1,0:T(8,128)(2,1)} %get-tuple-element.132.dq_ref, bf16[2048,192]{1,0:T(8,128)(2,1)} %get-tuple-element.134.dk_ref, bf16[2048,192]{1,0:T(8,128)(2,1)} %get-tuple-element.135.dv_ref, bf16[3,192,768]{2,1,0:T(8,128)(2,1)} %bitcast.19), custom_call_target="tpu_custom_call" | custom-call | flops 4 | bytes 4 | tf_op jit(solution)/shard_map/first_grad/pallas_call | solution.py:490
  185.0 7.6 %norm_one.1 = (bf16[1024,768]{1,0:T(8,128)(2,1)}, f32[8,768]{1,0:T(8,128)}) custom-call(s32[8]{0:T(128)} %and_select_fusion.half_ref.place_ref.table_ref, bf16[2048,192]{1,0:T(8,128)(2,1)} %get-tuple-element.132.dq_ref, bf16[2048,192]{1,0:T(8,128)(2,1)} %get-tuple-element.134.dk_ref, bf16[2048,192]{1,0:T(8,128)(2,1)} %get-tuple-element.135.dv_ref, ...), custom_call_target="tpu_custom_call" | custom-call | flops 10 | bytes 10 | tf_op jit(solution)/shard_map/norm_one/pallas_call | solution.py:523
  198.7 3.0 collective-permute-start.19
  213.4 10.3 %collective-permute-done.19.refs_2_ = bf16[192,768]{1,0:T(8,128)(2,1)S(1)} collective-permute-done((bf16[192,768]{1,0:T(8,128)(2,1)S(1)}, bf16[192,768]{1,0:T(8,128)(2,1)S(1)}, u32[]{:S(2)}, u32[]{:S(2)}) %collective-permute-start.19) | collective-permute-done | bytes 294944 | tf_op jit(solution)/shard_map/ppermute | solution.py:632
  226.8 3.4 %collective-permute-start.22 = (bf16[96,768]{1,0:T(8,128)(2,1)}, bf16[96,768]{1,0:T(8,128)(2,1)S(1)}, u32[]{:S(2)}, u32[]{:S(2)}) collective-permute-start(bf16[96,768]{1,0:T(8,128)(2,1)} %get-tuple-element.142), channel_id=1, source_target_pairs={{0,16},{4,20},{8,24},{12,28},{16,0},{20,4},{24,8},{28,12},{1,17},{... | collective-permute-start | bytes 442376 | tf_op jit(solution)/shard_map/ppermute | solution.py:632
  230.2 8.4 %collective-permute-done.20 = f32[8,768]{1,0:T(8,128)S(1)} collective-permute-done((f32[8,768]{1,0:T(8,128)S(1)}, f32[8,768]{1,0:T(8,128)S(1)}, u32[]{:S(2)}, u32[]{:S(2)}) %collective-permute-start.20) | collective-permute-done | bytes 24608 | tf_op jit(solution)/shard_map/ppermute | solution.py:632
  252.9 3.6 %constant_dynamic-update-slice_fusion.1 = (bf16[2048,768]{1,0:T(8,128)(2,1)S(1)}, bf16[1024,768]{1,0:T(8,128)(2,1)}) fusion(bf16[2048,768]{1,0:T(8,128)(2,1)S(1)} %broadcast.18.clone.1, s32[]{:T(128)S(6)} %select_n.54, bf16[1024,768]{1,0:T(8,128)(2,1)} %collective-permute-done.26, bf16[1024,768]{1,0:T(8,128)(2,1)} %get-tuple-element.130), kind=kLoop, calls=%fused_computation.39 | loop fusion | flops 3145728 | bytes 6291460 | tf_op jit(solution)/shard_map/dynamic_update_slice | solution.py:683
  258.9 7.6 %collective-permute-done.29.refs_1_ = bf16[48,768]{1,0:T(8,128)(2,1)S(1)} collective-permute-done((bf16[48,768]{1,0:T(8,128)(2,1)S(1)}, bf16[48,768]{1,0:T(8,128)(2,1)S(1)}, u32[]{:S(2)}, u32[]{:S(2)}) %collective-permute-start.29) | collective-permute-done | bytes 73760 | tf_op jit(solution)/shard_map/ppermute | solution.py:632
  270.2 3.1 collective-permute-start.32
  273.3 4.9 %collective-permute-done.31.refs_1_ = bf16[96,768]{1,0:T(8,128)(2,1)S(1)} collective-permute-done((bf16[96,768]{1,0:T(8,128)(2,1)}, bf16[96,768]{1,0:T(8,128)(2,1)S(1)}, u32[]{:S(2)}, u32[]{:S(2)}) %collective-permute-start.31) | collective-permute-done | bytes 147488 | tf_op jit(solution)/shard_map/ppermute | solution.py:632
  278.2 3.9 %collective-permute-done.32.refs_3_ = bf16[96,768]{1,0:T(8,128)(2,1)S(1)} collective-permute-done((bf16[96,768]{1,0:T(8,128)(2,1)}, bf16[96,768]{1,0:T(8,128)(2,1)S(1)}, u32[]{:S(2)}, u32[]{:S(2)}) %collective-permute-start.32) | collective-permute-done | bytes 147488 | tf_op jit(solution)/shard_map/ppermute | solution.py:632
  289.7 20.2 %all-reduce.3.cloned.1.call-done = (bf16[768,768]{1,0:T(8,128)(2,1)}, bf16[768,768]{1,0:T(8,128)(2,1)}) async-done(((bf16[768,768]{1,0:T(8,128)(2,1)}, bf16[768,768]{1,0:T(8,128)(2,1)}), (bf16[768,768]{1,0:T(8,128)(2,1)}, bf16[768,768]{1,0:T(8,128)(2,1)})) %all-reduce.3.cloned.1.call-update) | async-done | bytes 2359312 | tf_op jit(solution)/shard_map/psum | solution.py:742
  (186 shorter events, 102.5 us)
Async XLA Ops:
  7.2 302.7 %all-reduce.3.cloned.1.call-start = ((), (), s32[]{:S(2)}) async-start(), calls=%async_computation | async-start | bytes 4718592 | tf_op jit(solution)/shard_map/psum | solution.py:742
  7.2 10.3 %collective-permute-start.1 = (bf16[192,768]{1,0:T(8,128)(2,1)}, bf16[192,768]{1,0:T(8,128)(2,1)S(1)}, u32[]{:S(2)}, u32[]{:S(2)}) collective-permute-start(bf16[192,768]{1,0:T(8,128)(2,1)} %w0.5), channel_id=1, source_target_pairs={{0,2},{1,3},{2,0},{3,1},{4,6},{5,7},{6,4},{7,5},{8,10},{9,11},{10,... | collective-permute-start | bytes 884744 | tf_op jit(solution)/shard_map/ppermute | solution.py:672
  10.3 36.5 %collective-permute-start = (bf16[192,768]{1,0:T(8,128)(2,1)}, bf16[192,768]{1,0:T(8,128)(2,1)S(1)}, u32[]{:S(2)}, u32[]{:S(2)}) collective-permute-start(bf16[192,768]{1,0:T(8,128)(2,1)} %w0.5), channel_id=1, source_target_pairs={{0,1},{1,0},{2,3},{3,2},{4,5},{5,4},{6,7},{7,6},{8,9},{9,8},{10,11... | collective-permute-start | bytes 884744 | tf_op jit(solution)/shard_map/ppermute | solution.py:672
  17.5 29.3 %collective-permute-start.2 = (bf16[192,768]{1,0:T(8,128)(2,1)S(1)}, bf16[192,768]{1,0:T(8,128)(2,1)S(1)}, u32[]{:S(2)}, u32[]{:S(2)}) collective-permute-start(bf16[192,768]{1,0:T(8,128)(2,1)S(1)} %collective-permute-done.1.w2), channel_id=1, source_target_pairs={{0,1},{1,0},{2,3},{3,2},{4,5},{5,4},{6,7},{7,6},{8,9},{9,8},{10,11... | collective-permute-start | bytes 884744 | tf_op jit(solution)/shard_map/ppermute | solution.py:672
  46.8 20.2 %collective-permute-start.4 = (bf16[192,2048]{1,0:T(8,128)(2,1)}, bf16[192,2048]{1,0:T(8,128)(2,1)S(1)}, u32[]{:S(2)}, u32[]{:S(2)}) collective-permute-start(bf16[192,2048]{1,0:T(8,128)(2,1)} %get-tuple-element.95.a0.att_ref), channel_id=1, source_target_pairs={{0,2},{1,3},{2,0},{3,1},{4,6},{5,7},{6,4},{7,5},{8,10},{9,11},{10,... | collective-permute-start | bytes 2359304 | tf_op jit(solution)/shard_map/ppermute | solution.py:672
  48.6 19.2 %collective-permute-start.3 = (bf16[192,2048]{1,0:T(8,128)(2,1)}, bf16[192,2048]{1,0:T(8,128)(2,1)S(1)}, u32[]{:S(2)}, u32[]{:S(2)}) collective-permute-start(bf16[192,2048]{1,0:T(8,128)(2,1)} %get-tuple-element.95.a0.att_ref), channel_id=1, source_target_pairs={{0,1},{1,0},{2,3},{3,2},{4,5},{5,4},{6,7},{7,6},{8,9},{9,8},{10,11... | collective-permute-start | bytes 2359304 | tf_op jit(solution)/shard_map/ppermute | solution.py:672
  85.2 15.6 %collective-permute-start.6 = (bf16[1024,768]{1,0:T(8,128)(2,1)}, bf16[1024,768]{1,0:T(8,128)(2,1)S(1)}, u32[]{:S(2)}, u32[]{:S(2)}) collective-permute-start(bf16[1024,768]{1,0:T(8,128)(2,1)} %get-tuple-element.103), channel_id=1, source_target_pairs={{0,1},{1,0},{2,3},{3,2},{4,5},{5,4},{6,7},{7,6},{8,9},{9,8},{10,11... | collective-permute-start | bytes 4718600 | tf_op jit(solution)/shard_map/ppermute | solution.py:672
  85.4 41.4 %collective-permute-start.8 = (bf16[1024,768]{1,0:T(8,128)(2,1)}, bf16[1024,768]{1,0:T(8,128)(2,1)}, u32[]{:S(2)}, u32[]{:S(2)}) collective-permute-start(bf16[1024,768]{1,0:T(8,128)(2,1)} %get-tuple-element.111), channel_id=1, source_target_pairs={{0,1},{1,0},{2,3},{3,2},{4,5},{5,4},{6,7},{7,6},{8,9},{9,8},{10,11... | collective-permute-start | bytes 4718600 | tf_op jit(solution)/shard_map/ppermute | solution.py:672
  113.5 15.7 %collective-permute-start.10 = (bf16[192,768]{1,0:T(8,128)(2,1)}, bf16[192,768]{1,0:T(8,128)(2,1)}, u32[]{:S(2)}, u32[]{:S(2)}) collective-permute-start(bf16[192,768]{1,0:T(8,128)(2,1)} %convolution_convert_fusion.5), channel_id=1, source_target_pairs={{0,1},{1,0},{2,3},{3,2},{4,5},{5,4},{6,7},{7,6},{8,9},{9,8},{10,11... | collective-permute-start | bytes 884744 | tf_op jit(solution)/shard_map/ppermute | solution.py:672
  114.1 17.3 %collective-permute-start.9 = (bf16[192,768]{1,0:T(8,128)(2,1)S(1)}, bf16[192,768]{1,0:T(8,128)(2,1)}, u32[]{:S(2)}, u32[]{:S(2)}) collective-permute-start(bf16[192,768]{1,0:T(8,128)(2,1)S(1)} %convolution_convert_fusion.7), channel_id=1, source_target_pairs={{0,1},{1,0},{2,3},{3,2},{4,5},{5,4},{6,7},{7,6},{8,9},{9,8},{10,11... | collective-permute-start | bytes 884744 | tf_op jit(solution)/shard_map/ppermute | solution.py:672
  114.5 19.9 %collective-permute-start.7 = (bf16[384,1024]{1,0:T(8,128)(2,1)}, bf16[384,1024]{1,0:T(8,128)(2,1)}, u32[]{:S(2)}, u32[]{:S(2)}) collective-permute-start(bf16[384,1024]{1,0:T(8,128)(2,1)} %get-tuple-element.109), channel_id=1, source_target_pairs={{0,2},{1,3},{2,0},{3,1},{4,6},{5,7},{6,4},{7,5},{8,10},{9,11},{10,... | collective-permute-start | bytes 2359304 | tf_op jit(solution)/shard_map/ppermute | solution.py:672
  136.6 36.8 %collective-permute-start.12 = (bf16[1024,768]{1,0:T(8,128)(2,1)S(1)}, bf16[1024,768]{1,0:T(8,128)(2,1)S(1)}, u32[]{:S(2)}, u32[]{:S(2)}) collective-permute-start(bf16[1024,768]{1,0:T(8,128)(2,1)S(1)} %add_convert_fusion.2), channel_id=1, source_target_pairs={{0,2},{1,3},{2,0},{3,1},{4,6},{5,7},{6,4},{7,5},{8,10},{9,11},{10,... | collective-permute-start | bytes 4718600 | tf_op jit(solution)/shard_map/ppermute | solution.py:672
  180.3 12.4 %collective-permute-start.14 = (bf16[192,768]{1,0:T(8,128)(2,1)S(1)}, bf16[192,768]{1,0:T(8,128)(2,1)}, u32[]{:S(2)}, u32[]{:S(2)}) collective-permute-start(bf16[192,768]{1,0:T(8,128)(2,1)S(1)} %copy-done.25), channel_id=1, source_target_pairs={{0,2},{1,3},{2,0},{3,1},{4,6},{5,7},{6,4},{7,5},{8,10},{9,11},{10,... | collective-permute-start | bytes 884744 | tf_op jit(solution)/shard_map/ppermute | solution.py:672
  192.7 60.0 %collective-permute-start.26 = (bf16[1024,768]{1,0:T(8,128)(2,1)}, bf16[1024,768]{1,0:T(8,128)(2,1)}, u32[]{:S(2)}, u32[]{:S(2)}) collective-permute-start(bf16[1024,768]{1,0:T(8,128)(2,1)} %get-tuple-element.130), channel_id=1, source_target_pairs={{0,2},{1,3},{2,0},{3,1},{4,6},{5,7},{6,4},{7,5},{8,10},{9,11},{10,... | collective-permute-start | bytes 4718600 | tf_op jit(solution)/shard_map/ppermute | solution.py:672
  198.7 25.0 %collective-permute-start.19 = (bf16[192,768]{1,0:T(8,128)(2,1)S(1)}, bf16[192,768]{1,0:T(8,128)(2,1)S(1)}, u32[]{:S(2)}, u32[]{:S(2)}) collective-permute-start(bf16[192,768]{1,0:T(8,128)(2,1)S(1)} %fusion.9), channel_id=1, source_target_pairs={{0,8},{4,12},{8,0},{12,4},{16,24},{20,28},{24,16},{28,20},{1,9},{5... | collective-permute-start | bytes 884744 | tf_op jit(solution)/shard_map/ppermute | solution.py:632
  203.6 20.1 %collective-permute-start.18 = (bf16[192,768]{1,0:T(8,128)(2,1)S(1)}, bf16[192,768]{1,0:T(8,128)(2,1)S(1)}, u32[]{:S(2)}, u32[]{:S(2)}) collective-permute-start(bf16[192,768]{1,0:T(8,128)(2,1)S(1)} %fusion.10), channel_id=1, source_target_pairs={{0,4},{4,0},{8,12},{12,8},{16,20},{20,16},{24,28},{28,24},{1,5},{5... | collective-permute-start | bytes 884744 | tf_op jit(solution)/shard_map/ppermute | solution.py:632
  209.0 107.3 %collective-permute-start.13 = (bf16[1024,768]{1,0:T(8,128)(2,1)}, bf16[1024,768]{1,0:T(8,128)(2,1)}, u32[]{:S(2)}, u32[]{:S(2)}) collective-permute-start(bf16[1024,768]{1,0:T(8,128)(2,1)} %get-tuple-element.179), channel_id=1, source_target_pairs={{0,1},{1,0},{2,3},{3,2},{4,5},{5,4},{6,7},{7,6},{8,9},{9,8},{10,11... | collective-permute-start | bytes 4718600 | tf_op jit(solution)/shard_map/ppermute | solution.py:672
  226.8 11.8 %collective-permute-start.21 = (bf16[96,768]{1,0:T(8,128)(2,1)}, bf16[96,768]{1,0:T(8,128)(2,1)S(1)}, u32[]{:S(2)}, u32[]{:S(2)}) collective-permute-start(bf16[96,768]{1,0:T(8,128)(2,1)} %get-tuple-element.141), channel_id=1, source_target_pairs={{0,8},{4,12},{8,0},{12,4},{16,24},{20,28},{24,16},{28,20},{1,9},{5... | collective-permute-start | bytes 442376 | tf_op jit(solution)/shard_map/ppermute | solution.py:632
  226.8 12.0 %collective-permute-start.22 = (bf16[96,768]{1,0:T(8,128)(2,1)}, bf16[96,768]{1,0:T(8,128)(2,1)S(1)}, u32[]{:S(2)}, u32[]{:S(2)}) collective-permute-start(bf16[96,768]{1,0:T(8,128)(2,1)} %get-tuple-element.142), channel_id=1, source_target_pairs={{0,16},{4,20},{8,24},{12,28},{16,0},{20,4},{24,8},{28,12},{1,17},{... | collective-permute-start | bytes 442376 | tf_op jit(solution)/shard_map/ppermute | solution.py:632
  256.6 70.0 %collective-permute-start.27 = (bf16[1024,768]{1,0:T(8,128)(2,1)}, bf16[1024,768]{1,0:T(8,128)(2,1)}, u32[]{:S(2)}, u32[]{:S(2)}) collective-permute-start(bf16[1024,768]{1,0:T(8,128)(2,1)} %get-tuple-element.177), channel_id=1, source_target_pairs={{0,1},{1,0},{2,3},{3,2},{4,5},{5,4},{6,7},{7,6},{8,9},{9,8},{10,11... | collective-permute-start | bytes 4718600 | tf_op jit(solution)/shard_map/ppermute | solution.py:672
  256.6 9.9 %collective-permute-start.29 = (bf16[48,768]{1,0:T(8,128)(2,1)S(1)}, bf16[48,768]{1,0:T(8,128)(2,1)S(1)}, u32[]{:S(2)}, u32[]{:S(2)}) collective-permute-start(bf16[48,768]{1,0:T(8,128)(2,1)S(1)} %copy-done.33), channel_id=1, source_target_pairs={{0,16},{4,20},{8,24},{12,28},{16,0},{20,4},{24,8},{28,12},{1,17},{... | collective-permute-start | bytes 221192 | tf_op jit(solution)/shard_map/ppermute | solution.py:632
  270.2 12.0 %collective-permute-start.32 = (bf16[96,768]{1,0:T(8,128)(2,1)}, bf16[96,768]{1,0:T(8,128)(2,1)S(1)}, u32[]{:S(2)}, u32[]{:S(2)}) collective-permute-start(bf16[96,768]{1,0:T(8,128)(2,1)} %get-tuple-element.163.refs_2_), channel_id=1, source_target_pairs={{0,16},{4,20},{8,24},{12,28},{16,0},{20,4},{24,8},{28,12},{1,17},{... | collective-permute-start | bytes 442376 | tf_op jit(solution)/shard_map/ppermute | solution.py:632
  284.8 34.7 %collective-permute-start.33 = (bf16[192,768]{1,0:T(8,128)(2,1)}, bf16[192,768]{1,0:T(8,128)(2,1)S(1)}, u32[]{:S(2)}, u32[]{:S(2)}) collective-permute-start(bf16[192,768]{1,0:T(8,128)(2,1)} %get-tuple-element.164.refs_0_), channel_id=1, source_target_pairs={{0,4},{4,0},{8,12},{12,8},{16,20},{20,16},{24,28},{28,24},{1,5},{5... | collective-permute-start | bytes 884744 | tf_op jit(solution)/shard_map/ppermute | solution.py:632
  287.5 32.1 %collective-permute-start.34 = (bf16[192,768]{1,0:T(8,128)(2,1)}, bf16[192,768]{1,0:T(8,128)(2,1)}, u32[]{:S(2)}, u32[]{:S(2)}) collective-permute-start(bf16[192,768]{1,0:T(8,128)(2,1)} %get-tuple-element.165.refs_2_), channel_id=1, source_target_pairs={{0,8},{4,12},{8,0},{12,4},{16,24},{20,28},{24,16},{28,20},{1,9},{5... | collective-permute-start | bytes 884744 | tf_op jit(solution)/shard_map/ppermute | solution.py:632
  (55 other events, 292.9 us)
Sparse Core Ops, SparseCore 0:
  182.2 127.6 all-reduce.2
